TPU v7x, 768 devices: a whole 4x8x12 slice. The times are simulated.
768 devices in a mesh: mp: 48 (over z_hi, y, core), ens: 16 (over x, z_lo).
Axes of the slice: x: 4, y: 8, z: 12 (z_hi: 3, z_lo: 4; z = z_hi * 4 + z_lo), core: 2. Of those that a mesh axis runs over, the one named last changes fastest.
Arguments:
- ensemble: bfloat16 [192, 16, 16, 288], P('mp', 'ens'), may hold values from -1 to 1
- control: bfloat16 [192, 16, 16, 288], P(None, 'ens', None, 'mp'), may hold values from -6 to 6
- band: int32 [192], replicated, may hold values from 4 to 32
- wind_east: bfloat16 [192, 16, 288], P('mp'), may hold values from -0.44921875 to 0.44921875
- wind_north: bfloat16 [192, 16, 288], P('mp'), may hold values from -0.44921875 to 0.44921875
- observation_longitude: int32 [4, 192, 128], P(None, 'mp'), may hold values from 0 to 287
- innovation: float32 [4, 192, 16, 128], P(None, 'mp'), may hold values from -6 to 6
- observation_weight: float32 [4, 192, 128], P(None, 'mp'), may hold values from 0.25 to 4
Outputs:
- gradient: float32 [192, 16, 16, 288], P(None, 'ens', None, 'mp')
- departures: float32 [4, 192, 16, 128], P(None, 'mp', 'ens')
All inputs are finite; a program needn't handle non-finite values.
Results may differ from a plain program's by a relative error of at most 0.0027.
Values may be sent and summed in bfloat16 or wider, within the bound.
A program may use at most 32 MiB of HBM per device.

v0:
```python
import jax
import jax.numpy as jnp
from jax import lax
from jax.sharding import PartitionSpec as P


def padded(block, sides, width):
    for axis, dim in sides:
        count = lax.axis_size(axis)
        forward = [(i, i + 1) for i in range(count - 1)]
        backward = [(target, source) for source, target in forward]
        low = lax.ppermute(
            lax.slice_in_dim(block, block.shape[dim] - width, None, axis=dim), axis, forward
        )
        high = lax.ppermute(lax.slice_in_dim(block, 0, width, axis=dim), axis, backward)
        block = jnp.concatenate([low, block, high], axis=dim)
    return block


def from_everyone(array, axis):
    count = lax.axis_size(axis)
    return lax.all_to_all(
        jnp.broadcast_to(array[None], (count, *array.shape)), axis, 0, 0, tiled=True
    )


def taken_together(array, axis):
    everything = from_everyone(array, axis)
    return jnp.sum(everything, axis=0)


def localization(band):
    row_count = band.shape[0]
    latitude = jnp.arange(row_count, dtype=jnp.float32)
    widths = band.astype(jnp.float32)
    distance = jnp.abs(latitude[:, None] - latitude[None, :])
    return jnp.maximum(0.0, 1.0 - 2.0 * distance / (widths[:, None] + widths[None, :])).astype(
        jnp.bfloat16
    )


def apply_rows(kernel, quantity):
    shaped = quantity.reshape(quantity.shape[0], -1)
    return jnp.dot(kernel, shaped, preferred_element_type=jnp.float32).reshape(quantity.shape)


def coefficients(wind_east, wind_north):
    return (
        1.0 - jnp.abs(wind_east) - jnp.abs(wind_north),
        jnp.maximum(wind_east, 0.0),
        jnp.maximum(-wind_east, 0.0),
        jnp.maximum(wind_north, 0.0),
        jnp.maximum(-wind_north, 0.0),
    )


def below(quantity):
    zero_row = jnp.zeros_like(quantity[:1])
    return jnp.concatenate([zero_row, quantity[:-1]], axis=0)


def above(quantity):
    zero_row = jnp.zeros_like(quantity[:1])
    return jnp.concatenate([quantity[1:], zero_row], axis=0)


def forward_local(quantity, coeffs):
    center, from_west, from_east, from_south, from_north = coeffs
    result = (
        center * quantity
        + from_west * jnp.roll(quantity, 1, axis=2)
        + from_east * jnp.roll(quantity, -1, axis=2)
    )
    return result + from_south * below(quantity) + from_north * above(quantity)


def adjoint_local(quantity, coeffs):
    center, from_west, from_east, from_south, from_north = coeffs
    result = (
        center * quantity
        + jnp.roll(from_west * quantity, -1, axis=2)
        + jnp.roll(from_east * quantity, 1, axis=2)
    )
    return result + above(from_south * quantity) + below(from_north * quantity)


def selector(lon_index, count):
    columns = jnp.arange(count, dtype=jnp.int32)
    return (lon_index[:, :, None] == columns[None, None, :]).astype(jnp.float32)


def sample(quantity, lon_index):
    picks = selector(lon_index, quantity.shape[2])
    return jnp.einsum("ilk,iok->ilo", quantity, picks, precision=lax.Precision.HIGHEST)


def inject(quantity, lon_index, amounts):
    picks = selector(lon_index, quantity.shape[2])
    return quantity + jnp.einsum("ilo,iok->ilk", amounts, picks, precision=lax.Precision.HIGHEST)


def margin_sweep(
    increment, wind_east, wind_north, observation_longitude, innovation, observation_weight
):
    depth = observation_longitude.shape[0]
    rows = increment.shape[0]
    fields = jnp.stack([increment, wind_east.astype(jnp.float32), wind_north.astype(jnp.float32)])
    widened = padded(fields, (("mp", 1),), depth)
    coeffs = coefficients(widened[1], widened[2])
    quantity = widened[0]
    departures = []
    for moment_value in range(depth):
        quantity = forward_local(quantity, coeffs)
        departures.append(
            sample(quantity[depth : depth + rows], observation_longitude[moment_value])
            - innovation[moment_value]
        )
    stacked = jnp.stack(departures)
    weighted = observation_weight[:, :, None, :] * stacked
    sources = jnp.concatenate(
        [weighted, observation_longitude[:, :, None, :].astype(jnp.float32)], axis=2
    )
    wide_sources = padded(sources, (("mp", 1),), depth)
    amounts = wide_sources[:, :, :-1]
    longitudes = wide_sources[:, :, -1].astype(jnp.int32)
    sensitivity = jnp.zeros_like(quantity)
    for moment_value in reversed(range(depth)):
        sensitivity = inject(sensitivity, longitudes[moment_value], amounts[moment_value])
        sensitivity = adjoint_local(sensitivity, coeffs)
    return (sensitivity[depth : depth + rows], stacked)


def run_sweep(
    increment, wind_east, wind_north, observation_longitude, innovation, observation_weight
):
    return margin_sweep(
        increment, wind_east, wind_north, observation_longitude, innovation, observation_weight
    )


def shards(
    ensemble,
    control,
    band,
    wind_east,
    wind_north,
    observation_longitude,
    innovation,
    observation_weight,
):
    kernel = localization(band)
    spread = apply_rows(kernel, control).astype(jnp.bfloat16)
    tile_field = lax.all_to_all(spread, "mp", split_axis=0, concat_axis=3, tiled=True)
    partial_value = jnp.sum(ensemble.astype(jnp.float32) * tile_field.astype(jnp.float32), axis=1)
    level_share = innovation.shape[2] // lax.axis_size("ens")
    first_level = lax.axis_index("ens") * level_share
    increment = taken_together(partial_value, "ens")
    sensitivity, all_departures = run_sweep(
        increment, wind_east, wind_north, observation_longitude, innovation, observation_weight
    )
    departures = lax.dynamic_slice_in_dim(all_departures, first_level, level_share, 2)
    product = (ensemble.astype(jnp.float32) * sensitivity[:, None]).astype(jnp.bfloat16)
    row_blocks = lax.all_to_all(product, "mp", split_axis=3, concat_axis=0, tiled=True)
    gradient = apply_rows(kernel, row_blocks) + control.astype(jnp.float32)
    return (gradient, departures)


def solution(mesh):
    placed = (
        P("mp", "ens", None, None),
        P(None, "ens", None, "mp"),
        P(),
        P("mp", None, None),
        P("mp", None, None),
        P(None, "mp", None),
        P(None, "mp", None, None),
        P(None, "mp", None),
    )
    return jax.shard_map(
        shards,
        mesh=mesh,
        in_specs=placed,
        out_specs=(P(None, "ens", None, "mp"), P(None, "mp", "ens", None)),
        check_vma=False,
    )
```

profile of v0, /device:TPU:1, one launch (start us, length us, event | category | flops | bytes accessed | tf_op | source)
XLA Modules:
  0.0 156.9 jit_solution(9363446685024363243)
XLA Ops:
  0.6 0.7 convert_element_type.62
  1.3 0.8 copy.45
  3.0 32.9 %all_to_all.29 = bf16[48,2,192]{2,1,0:T(2,128)(2,1)S(1)} all-to-all(bf16[48,2,192]{2,1,0:T(2,128)(2,1)S(1)} %reshape.87), channel_id=1, replica_groups=mesh['mp'=48,'ens'=16] {'mp'}, dimensions={0} | all-to-all | bytes 73728 | tf_op jit(solution)/shard_map/all_to_all | solution.py:153
  37.0 1.4 broadcast_in_dim.7
  38.4 7.2 %all-to-all-start.1 = ((f32[16,4,16,288]{3,2,1,0:T(8,128)}), f32[16,4,16,288]{3,2,1,0:T(8,128)S(1)}, u32[]{:S(2)}, u32[]{:S(2)}) async-start(f32[16,4,16,288]{3,2,1,0:T(8,128)} %broadcast_in_dim.7), calls=%async_computation.1 | async-start | bytes 3145728 | tf_op jit(solution)/shard_map/all_to_all | solution.py:22
  45.7 38.5 %all-to-all-done.1 = f32[16,4,16,288]{3,2,1,0:T(8,128)S(1)} async-done(((f32[16,4,16,288]{3,2,1,0:T(8,128)}), f32[16,4,16,288]{3,2,1,0:T(8,128)S(1)}, u32[]{:S(2)}, u32[]{:S(2)}) %all-to-all-start.1) | async-done | bytes 1179680 | tf_op jit(solution)/shard_map/all_to_all | solution.py:22
  84.3 3.3 %collective-permute-start.1 = (f32[3,4,16,288]{3,2,1,0:T(8,128)S(1)}, f32[3,4,16,288]{3,2,1,0:T(8,128)S(1)}, u32[]{:S(2)}, u32[]{:S(2)}) collective-permute-start(f32[3,4,16,288]{3,2,1,0:T(8,128)S(1)} %pad_maximum_fusion.1), channel_id=1, source_target_pairs={{16,0},{32,16},{48,32},{64,48},{80,64},{96,80},{112,96},{128,112},... | collective-permute-start | bytes 663560 | tf_op jit(solution)/shard_map/ppermute | solution.py:15
  87.6 2.5 %collective-permute-start = (f32[3,4,16,288]{3,2,1,0:T(8,128)S(1)}, f32[3,4,16,288]{3,2,1,0:T(8,128)S(1)}, u32[]{:S(2)}, u32[]{:S(2)}) collective-permute-start(f32[3,4,16,288]{3,2,1,0:T(8,128)S(1)} %pad_maximum_fusion.1), channel_id=1, source_target_pairs={{0,16},{16,32},{32,48},{48,64},{64,80},{80,96},{96,112},{112,128},... | collective-permute-start | bytes 663560 | tf_op jit(solution)/shard_map/ppermute | solution.py:12
  90.1 2.5 %collective-permute-done.1 = f32[3,4,16,288]{3,2,1,0:T(8,128)S(1)} collective-permute-done((f32[3,4,16,288]{3,2,1,0:T(8,128)S(1)}, f32[3,4,16,288]{3,2,1,0:T(8,128)S(1)}, u32[]{:S(2)}, u32[]{:S(2)}) %collective-permute-start.1) | collective-permute-done | bytes 221216 | tf_op jit(solution)/shard_map/ppermute | solution.py:15
  92.6 1.2 collective-permute-done
  97.9 1.9 %collective-permute-start.3 = (f32[4,4,17,128]{3,2,1,0:T(8,128)S(1)}, f32[4,4,17,128]{3,2,1,0:T(8,128)S(1)}, u32[]{:S(2)}, u32[]{:S(2)}) collective-permute-start(f32[4,4,17,128]{3,2,1,0:T(8,128)S(1)} %pad_maximum_fusion.2), channel_id=1, source_target_pairs={{16,0},{32,16},{48,32},{64,48},{80,64},{96,80},{112,96},{128,112},... | collective-permute-start | bytes 417800 | tf_op jit(solution)/shard_map/ppermute | solution.py:15
  99.8 4.4 %collective-permute-start.2 = (f32[4,4,17,128]{3,2,1,0:T(8,128)S(1)}, f32[4,4,17,128]{3,2,1,0:T(8,128)S(1)}, u32[]{:S(2)}, u32[]{:S(2)}) collective-permute-start(f32[4,4,17,128]{3,2,1,0:T(8,128)S(1)} %pad_maximum_fusion.2), channel_id=1, source_target_pairs={{0,16},{16,32},{32,48},{48,64},{64,80},{80,96},{96,112},{112,128},... | collective-permute-start | bytes 417800 | tf_op jit(solution)/shard_map/ppermute | solution.py:12
  104.2 1.4 collective-permute-done.3
  105.6 1.2 collective-permute-done.2
  106.9 1.0 bitcast_multiply_fusion.3
  108.1 1.0 bitcast_multiply_fusion.2
  109.4 1.0 bitcast_multiply_fusion.1
  110.7 1.0 bitcast_multiply_fusion.4
  112.4 0.9 reshape.89
  113.2 28.4 %all-to-all-start.2 = ((bf16[48,2,192]{2,1,0:T(2,128)(2,1)}), bf16[48,2,192]{2,1,0:T(2,128)(2,1)S(1)}, u32[]{:S(2)}, u32[]{:S(2)}) async-start(bf16[48,2,192]{2,1,0:T(2,128)(2,1)} %reshape.89), calls=%async_computation.2 | async-start | bytes 98304 | tf_op jit(solution)/shard_map/all_to_all | solution.py:163
  142.2 11.4 %all-to-all-done.2 = bf16[48,2,192]{2,1,0:T(2,128)(2,1)S(1)} async-done(((bf16[48,2,192]{2,1,0:T(2,128)(2,1)}), bf16[48,2,192]{2,1,0:T(2,128)(2,1)S(1)}, u32[]{:S(2)}, u32[]{:S(2)}) %all-to-all-start.2) | async-done | bytes 36896 | tf_op jit(solution)/shard_map/all_to_all | solution.py:163
  153.9 1.2 copy.53
  155.1 0.8 reshape.80
  156.0 0.9 fusion.7
  (81 shorter events, 8.5 us)
Async XLA Ops:
  36.2 0.8 copy-start
  38.4 7.3 %copy-start.5 = (s32[4,4,128]{2,1,0:T(4,128)S(1)}, s32[4,4,128]{2,1,0:T(4,128)}, u32[]{:S(2)}) copy-start(s32[4,4,128]{2,1,0:T(4,128)} %param.13) | copy-start | bytes 24580
  38.4 7.3 %copy-start.2 = (bf16[4,16,288]{2,1,0:T(8,128)(2,1)S(1)}, bf16[4,16,288]{2,1,0:T(8,128)(2,1)}, u32[]{:S(2)}) copy-start(bf16[4,16,288]{2,1,0:T(8,128)(2,1)} %param.12) | copy-start | bytes 110596
  38.4 7.3 %copy-start.3 = (bf16[4,16,288]{2,1,0:T(8,128)(2,1)S(1)}, bf16[4,16,288]{2,1,0:T(8,128)(2,1)}, u32[]{:S(2)}) copy-start(bf16[4,16,288]{2,1,0:T(8,128)(2,1)} %param.11) | copy-start | bytes 110596
  38.4 45.8 %all-to-all-start.1 = ((f32[16,4,16,288]{3,2,1,0:T(8,128)}), f32[16,4,16,288]{3,2,1,0:T(8,128)S(1)}, u32[]{:S(2)}, u32[]{:S(2)}) async-start(f32[16,4,16,288]{3,2,1,0:T(8,128)} %broadcast_in_dim.7), calls=%async_computation.1 | async-start | bytes 3145728 | tf_op jit(solution)/shard_map/all_to_all | solution.py:22
  84.3 8.3 %collective-permute-start.1 = (f32[3,4,16,288]{3,2,1,0:T(8,128)S(1)}, f32[3,4,16,288]{3,2,1,0:T(8,128)S(1)}, u32[]{:S(2)}, u32[]{:S(2)}) collective-permute-start(f32[3,4,16,288]{3,2,1,0:T(8,128)S(1)} %pad_maximum_fusion.1), channel_id=1, source_target_pairs={{16,0},{32,16},{48,32},{64,48},{80,64},{96,80},{112,96},{128,112},... | collective-permute-start | bytes 663560 | tf_op jit(solution)/shard_map/ppermute | solution.py:15
  87.6 6.1 %collective-permute-start = (f32[3,4,16,288]{3,2,1,0:T(8,128)S(1)}, f32[3,4,16,288]{3,2,1,0:T(8,128)S(1)}, u32[]{:S(2)}, u32[]{:S(2)}) collective-permute-start(f32[3,4,16,288]{3,2,1,0:T(8,128)S(1)} %pad_maximum_fusion.1), channel_id=1, source_target_pairs={{0,16},{16,32},{32,48},{48,64},{64,80},{80,96},{96,112},{112,128},... | collective-permute-start | bytes 663560 | tf_op jit(solution)/shard_map/ppermute | solution.py:12
  95.6 0.9 copy-start.1
  96.5 1.4 copy-start.6
  97.9 7.7 %collective-permute-start.3 = (f32[4,4,17,128]{3,2,1,0:T(8,128)S(1)}, f32[4,4,17,128]{3,2,1,0:T(8,128)S(1)}, u32[]{:S(2)}, u32[]{:S(2)}) collective-permute-start(f32[4,4,17,128]{3,2,1,0:T(8,128)S(1)} %pad_maximum_fusion.2), channel_id=1, source_target_pairs={{16,0},{32,16},{48,32},{64,48},{80,64},{96,80},{112,96},{128,112},... | collective-permute-start | bytes 417800 | tf_op jit(solution)/shard_map/ppermute | solution.py:15
  99.8 7.0 %collective-permute-start.2 = (f32[4,4,17,128]{3,2,1,0:T(8,128)S(1)}, f32[4,4,17,128]{3,2,1,0:T(8,128)S(1)}, u32[]{:S(2)}, u32[]{:S(2)}) collective-permute-start(f32[4,4,17,128]{3,2,1,0:T(8,128)S(1)} %pad_maximum_fusion.2), channel_id=1, source_target_pairs={{0,16},{16,32},{32,48},{48,64},{64,80},{80,96},{96,112},{112,128},... | collective-permute-start | bytes 417800 | tf_op jit(solution)/shard_map/ppermute | solution.py:12
  112.1 43.9 %copy-start.4 = (bf16[192,1,16,6]{0,2,3,1:T(8,128)(2,1)S(1)}, bf16[192,1,16,6]{0,2,3,1:T(8,128)(2,1)}, u32[]{:S(2)}) copy-start(bf16[192,1,16,6]{0,2,3,1:T(8,128)(2,1)} %param.9) | copy-start | bytes 110596
  113.2 40.4 %all-to-all-start.2 = ((bf16[48,2,192]{2,1,0:T(2,128)(2,1)}), bf16[48,2,192]{2,1,0:T(2,128)(2,1)S(1)}, u32[]{:S(2)}, u32[]{:S(2)}) async-start(bf16[48,2,192]{2,1,0:T(2,128)(2,1)} %reshape.89), calls=%async_computation.2 | async-start | bytes 98304 | tf_op jit(solution)/shard_map/all_to_all | solution.py:163
where the time goes:
time: 157 us
  waiting for transfers between devices  56.1 us (36%)
  starting transfers between devices  47.7 us (30%)
  blocking collectives  32.9 us (21%)
  local copies, waits for them, and re-layouts  10.5 us (7%)
  matrix products  6.36 us (4%)
  other arithmetic  2.16 us (1%)
    all_to_all x1, waiting for transfers between devices, from_everyone(): lax.all_to_all(jnp.broadcast_to(array[None], (count, *array.shape)), axis...  38.5 us
    all_to_all x1, blocking collectives, shards(): lax.all_to_all(spread, 'mp', split_axis=0, concat_axis=3, tiled=True)  32.9 us
    all_to_all x1, starting transfers between devices, shards(): lax.all_to_all(product, 'mp', split_axis=3, concat_axis=0, tiled=True)  28.4 us
    all_to_all x1, waiting for transfers between devices, shards(): lax.all_to_all(product, 'mp', split_axis=3, concat_axis=0, tiled=True)  11.4 us
    all_to_all x1, starting transfers between devices, from_everyone(): lax.all_to_all(jnp.broadcast_to(array[None], (count, *array.shape)), axis...  7.25 us
    ppermute x2, starting transfers between devices, padded(): lax.ppermute(lax.slice_in_dim(block, block.shape[dim] - width, None, axis...  6.86 us
    ppermute x2, starting transfers between devices, padded(): lax.ppermute(lax.slice_in_dim(block, 0, width, axis=dim), axis, backward)  5.22 us
    ppermute x2, waiting for transfers between devices, padded(): lax.ppermute(lax.slice_in_dim(block, 0, width, axis=dim), axis, backward)  3.86 us
  transfers between devices with their start and end apart: 6, of which 6 were waited for; matrix products, arithmetic and copies ran while one was open for 0% of the time, Pallas kernels for 0%

commit v1 on v0

v1 whole, which is shorter than its diff:
```python
import functools

import jax
import jax.numpy as jnp
from jax import lax
from jax.experimental import pallas as pl
from jax.experimental.pallas import tpu as pltpu
from jax.sharding import PartitionSpec as P

MESH = pl.DeviceIdType.MESH
MP, ENS = 48, 16
LAT, LEV, LON, OBS, SLOTS = 192, 16, 288, 128, 4
TILE = 4
KB = 6
WIDE = MP * 8
ROWS = 24
F32, BF16 = jnp.float32, jnp.bfloat16


def iota(shape, dim):
    return lax.broadcasted_iota(jnp.int32, shape, dim)


def split3(value):
    first = value.astype(BF16)
    rest = value - first.astype(F32)
    second = rest.astype(BF16)
    third = (rest - second.astype(F32)).astype(BF16)
    return first.astype(F32), second.astype(F32), third.astype(F32)


def body(
    ens_hbm, ctl_hbm, band_hbm, east_hbm, north_hbm, lon_hbm, inn_hbm, wgt_hbm,
    grad_hbm, dep_hbm,
    ens_v, ctl_v, band_v, east_v, north_v, lon_v, inn_v, wgt_v, grad_v, dep_v,
    kern_v, rows_v, wide_v, ensw_v, state_v,
    a1_send, a1_recv, part_v, rs_recv, inc_v, halo_recv,
    wind_own, wind_recv, db_own, db_recv, coef_v, dfull_v, bfull_v,
    ag_send, ag_recv, a2_send, a2_recv,
    in_sem, out_sem, send_sem, recv_sem,
):
    q = lax.axis_index("mp")
    e = lax.axis_index("ens")

    pairs = [
        (ctl_hbm, ctl_v), (band_hbm, band_v), (ens_hbm, ens_v), (east_hbm, east_v),
        (north_hbm, north_v), (lon_hbm, lon_v), (inn_hbm, inn_v), (wgt_hbm, wgt_v),
    ]
    loads = [
        pltpu.make_async_copy(src, dst, in_sem.at[n]) for n, (src, dst) in enumerate(pairs)
    ]
    for copy in loads:
        copy.start()
    barrier = pltpu.get_barrier_semaphore()

    def greet_mp(d, carry):
        pl.semaphore_signal(
            barrier, inc=1, device_id={"mp": (q + d) % MP}, device_id_type=MESH
        )
        return carry

    def greet_ens(d, carry):
        pl.semaphore_signal(
            barrier, inc=1, device_id={"ens": (e + d) % ENS}, device_id_type=MESH
        )
        return carry

    lax.fori_loop(1, MP, greet_mp, 0)
    lax.fori_loop(1, ENS, greet_ens, 0)

    part_v[...] = jnp.zeros_like(part_v)
    ag_send[...] = jnp.zeros_like(ag_send)
    state_v[...] = jnp.zeros_like(state_v)
    wide_v[...] = jnp.zeros_like(wide_v)
    dfull_v[...] = jnp.zeros_like(dfull_v)
    bfull_v[...] = jnp.zeros_like(bfull_v)

    loads[1].wait()
    width_j = jnp.broadcast_to(band_v[...].astype(F32), (LAT, LAT))
    width_i = width_j.T
    distance = jnp.abs(iota((LAT, LAT), 0) - iota((LAT, LAT), 1)).astype(F32)
    kern_v[...] = jnp.maximum(0.0, 1.0 - 2.0 * distance / (width_i + width_j)).astype(BF16)

    loads[0].wait()
    spread = lax.dot_general(
        kern_v[...], ctl_v[...], (((1,), (1,)), ((), ())), preferred_element_type=F32
    )
    rows_v[...] = jnp.concatenate([spread, jnp.zeros((LAT, 128 - KB * LEV), F32)], axis=1)
    group = iota((MP, 128), 1) >> 4
    by_row = [rows_v[pl.ds(i, MP, stride=TILE), :] for i in range(TILE)]
    for k in range(KB):
        block = jnp.zeros((MP, 128), F32)
        for i in range(TILE):
            block = jnp.where(group == i, pltpu.roll(by_row[i], (16 * (i - k)) % 128, 1), block)
        wide_v[pl.ds(k, MP, stride=8), :] = block
    a1_send[...] = wide_v[...].reshape(MP, 8, 128).astype(BF16)

    pl.semaphore_wait(barrier, MP + ENS - 2)

    def send_spread(d, carry):
        to = (q + d) % MP
        pltpu.make_async_remote_copy(
            src_ref=a1_send.at[to], dst_ref=a1_recv.at[q],
            send_sem=send_sem.at[0], recv_sem=recv_sem.at[0],
            device_id={"mp": to}, device_id_type=MESH,
        ).start()
        return carry

    lax.fori_loop(1, MP, send_spread, 0)
    pltpu.make_async_copy(a1_send.at[q], a1_recv.at[q], recv_sem.at[0]).start()

    source = iota((LON, WIDE), 1)
    embed = (
        (iota((LON, WIDE), 0) == (source >> 3) * 6 + (source & 7)) & ((source & 7) < KB)
    ).astype(F32).astype(BF16)
    for copy in loads[2:5]:
        copy.wait()
    ensw_v[...] = jnp.dot(ens_v[...], embed, preferred_element_type=F32)
    mine = iota((LEV, LON), 0) == e
    winds = []
    for ref in (east_v, north_v):
        for i in range(TILE):
            level = ref[LEV * i : LEV * (i + 1), :].astype(F32)
            winds.append(jnp.sum(jnp.where(mine, level, 0.0), axis=0, keepdims=True))
    wind_own[...] = jnp.dot(
        jnp.concatenate(winds, axis=0).astype(BF16), embed, preferred_element_type=F32
    )

    offsets = (-2, -1, 1, 2)

    def to_tiles(src, dst, slots, send, recv):
        for slot, offset in slots:
            pltpu.make_async_remote_copy(
                src_ref=src, dst_ref=dst.at[slot], send_sem=send, recv_sem=recv,
                device_id={"mp": (q - offset + MP) % MP}, device_id_type=MESH,
            ).start()

    to_tiles(wind_own, wind_recv, enumerate(offsets), send_sem.at[1], recv_sem.at[1])

    for copy in loads[5:]:
        copy.wait()
    own_level = iota((LEV, OBS), 0) == e
    lane_rows = iota((WIDE, OBS), 0)
    wide_lon = []
    observed = []
    for t in range(SLOTS):
        lon = lon_v[t]
        place = lon + 2 * ((lon * 10923) >> 16)
        wide_lon.append(place)
        weight = wgt_v[t]
        level_rows = []
        for i in range(TILE):
            start = LEV * (TILE * t + i)
            level_rows.append(
                jnp.sum(
                    jnp.where(own_level, inn_v[start : start + LEV, :], 0.0),
                    axis=0, keepdims=True,
                )
            )
        level_innovation = jnp.concatenate(level_rows, axis=0)
        observed.append(level_innovation)
        parts = split3(weight) + split3(weight * level_innovation)
        for i in range(TILE):
            hits = (lane_rows == place[i : i + 1, :]).astype(F32).astype(BF16)
            lhs = jnp.concatenate(
                [part[i : i + 1, :] for part in parts] + [jnp.zeros((2, OBS), F32)], axis=0
            ).astype(BF16)
            sums = lax.dot_general(
                lhs, hits, (((1,), (1,)), ((), ())), preferred_element_type=F32
            )
            at = TILE * t + i
            db_own[at : at + 1, :] = sums[0:1] + sums[1:2] + sums[2:3]
            db_own[16 + at : 17 + at, :] = sums[3:4] + sums[4:5] + sums[5:6]
    to_tiles(db_own, db_recv, ((0, -1), (1, 1)), send_sem.at[2], recv_sem.at[2])

    pltpu.make_async_copy(a1_recv, a1_recv, recv_sem.at[0]).wait()
    native = a1_recv[...].astype(F32).reshape(WIDE, 128).T
    for i in range(TILE):
        part = ensw_v[LEV * i : LEV * (i + 1), :] * native[LEV * i : LEV * (i + 1), :]
        for c in range(3):
            part_v[pl.ds(4 * c + i, LEV, stride=16), :] = part[:, 128 * c : 128 * (c + 1)]

    def send_part(d, carry):
        to = (e + d) % ENS
        pltpu.make_async_remote_copy(
            src_ref=part_v.at[pl.ds(pl.multiple_of(to * 16, 16), 16)], dst_ref=rs_recv.at[d - 1],
            send_sem=send_sem.at[3], recv_sem=recv_sem.at[3],
            device_id={"ens": to}, device_id_type=MESH,
        ).start()
        return carry

    lax.fori_loop(1, ENS, send_part, 0)

    pltpu.make_async_copy(wind_recv, wind_recv, recv_sem.at[1]).wait()
    pltpu.make_async_copy(db_recv, db_recv, recv_sem.at[2]).wait()
    row = iota((ROWS, WIDE), 0)
    globe = row + (TILE * q - 8)
    inside = (globe >= 0) & (globe < LAT) & (row < 20)
    slabs = [wind_recv[0], wind_recv[1], wind_own[...], wind_recv[2], wind_recv[3]]
    blank = jnp.zeros((TILE, WIDE), F32)
    east = jnp.concatenate([slab[0:4] for slab in slabs] + [blank], axis=0)
    north = jnp.concatenate([slab[4:8] for slab in slabs] + [blank], axis=0)
    coefs = (
        1.0 - jnp.abs(east) - jnp.abs(north),
        jnp.maximum(east, 0.0), jnp.maximum(-east, 0.0),
        jnp.maximum(north, 0.0), jnp.maximum(-north, 0.0),
    )
    for n, coef in enumerate(coefs):
        coef_v[n] = jnp.where(inside, coef, 0.0)
    for t in range(SLOTS):
        at = TILE * t
        for full, base in ((dfull_v, 0), (bfull_v, 16)):
            full[t, 4:8, :] = db_recv[0, base + at : base + at + 4, :]
            full[t, 8:12, :] = db_own[base + at : base + at + 4, :]
            full[t, 12:16, :] = db_recv[1, base + at : base + at + 4, :]

    own_part = part_v[pl.ds(pl.multiple_of(e * 16, 16), 16), :]
    pltpu.make_async_copy(rs_recv, rs_recv, recv_sem.at[3]).wait()
    total = own_part
    for d in range(ENS - 1):
        total = total + rs_recv[d]
    inc_v[...] = total
    to_tiles(inc_v, halo_recv, enumerate(offsets), send_sem.at[4], recv_sem.at[4])
    pltpu.make_async_copy(halo_recv, halo_recv, recv_sem.at[4]).wait()
    for s in range(5):
        for c in range(3):
            if s == 2:
                piece = inc_v[4 * c : 4 * c + 4, :]
            else:
                piece = halo_recv[s if s < 2 else s - 1, 4 * c : 4 * c + 4, :]
            state_v[0, 4 * s : 4 * s + 4, 128 * c : 128 * (c + 1)] = piece

    lane = iota((ROWS, WIDE), 1) & 7
    first, last = lane == 0, lane == KB - 1

    def west(value):
        return jnp.where(first, pltpu.roll(value, 3, 1), pltpu.roll(value, 1, 1))

    def east_of(value):
        return jnp.where(last, pltpu.roll(value, WIDE - 3, 1), pltpu.roll(value, WIDE - 1, 1))

    def below(value):
        return pltpu.roll(value, 1, 0)

    def above(value):
        return pltpu.roll(value, ROWS - 1, 0)

    center, from_west, from_east, from_south, from_north = [coef_v[n] for n in range(5)]
    quantity = jnp.where(inside, state_v[0], 0.0)
    for t in range(SLOTS):
        quantity = (
            center * quantity + from_west * west(quantity) + from_east * east_of(quantity)
            + from_south * below(quantity) + from_north * above(quantity)
        )
        state_v[t] = quantity
    sens = jnp.zeros((ROWS, WIDE), F32)
    for t in reversed(range(SLOTS)):
        sens = sens + (dfull_v[t] * state_v[t] - bfull_v[t])
        sens = (
            center * sens + east_of(from_west * sens) + west(from_east * sens)
            + above(from_south * sens) + below(from_north * sens)
        )

    for c in range(3):
        ag_send[4 * c : 4 * c + 4, :] = sens[8:12, 128 * c : 128 * (c + 1)]

    def send_level(d, carry):
        pltpu.make_async_remote_copy(
            src_ref=ag_send, dst_ref=ag_recv.at[e],
            send_sem=send_sem.at[5], recv_sem=recv_sem.at[5],
            device_id={"ens": (e + d) % ENS}, device_id_type=MESH,
        ).start()
        return carry

    lax.fori_loop(1, ENS, send_level, 0)
    pltpu.make_async_copy(ag_send, ag_recv.at[e], recv_sem.at[5]).start()

    for h in range(2):
        pair = jnp.concatenate([state_v[2 * h, 8:12, :], state_v[2 * h + 1, 8:12, :]], axis=0)
        place = jnp.concatenate(wide_lon[2 * h : 2 * h + 2], axis=0)
        within = place & 127
        sampled = jnp.zeros((8, OBS), F32)
        for c in range(3):
            picked = jnp.take_along_axis(pair[:, 128 * c : 128 * (c + 1)], within, axis=1)
            sampled = jnp.where((place >> 7) == c, picked, sampled)
        dep_v[8 * h : 8 * h + 8, :] = sampled - jnp.concatenate(observed[2 * h : 2 * h + 2], axis=0)
    dep_copy = pltpu.make_async_copy(dep_v, dep_hbm, out_sem.at[0])
    dep_copy.start()

    pltpu.make_async_copy(ag_recv, ag_recv, recv_sem.at[5]).wait()
    products = []
    for i in range(TILE):
        level = jnp.concatenate([ag_recv[:, 4 * c + i, :] for c in range(3)], axis=1)
        products.append(
            (ensw_v[LEV * i : LEV * (i + 1), :] * level).astype(BF16).astype(F32)
        )
    products.append(jnp.zeros((128 - TILE * LEV, WIDE), F32))
    wide_v[...] = jnp.concatenate(products, axis=0).T
    by_lon = [wide_v[pl.ds(k, MP, stride=8), :] for k in range(KB)]
    for i in range(TILE):
        block = jnp.zeros((MP, 128), F32)
        for k in range(KB):
            block = jnp.where(group == k, pltpu.roll(by_lon[k], (16 * (k - i)) % 128, 1), block)
        rows_v[pl.ds(i, MP, stride=TILE), :] = block
    a2_send[...] = rows_v[...].reshape(MP, TILE, 128).astype(BF16)

    def send_product(d, carry):
        to = (q + d) % MP
        pltpu.make_async_remote_copy(
            src_ref=a2_send.at[to], dst_ref=a2_recv.at[q],
            send_sem=send_sem.at[6], recv_sem=recv_sem.at[6],
            device_id={"mp": to}, device_id_type=MESH,
        ).start()
        return carry

    lax.fori_loop(1, MP, send_product, 0)
    pltpu.make_async_copy(a2_send.at[q], a2_recv.at[q], recv_sem.at[6]).start()

    def sent(ref, n):
        pltpu.make_async_copy(ref, ref, send_sem.at[n]).wait()

    sent(a1_send.at[pl.ds(0, MP - 1)], 0)
    sent(wind_recv, 1)
    sent(db_recv, 2)
    sent(rs_recv, 3)
    sent(halo_recv, 4)
    sent(ag_recv.at[pl.ds(0, ENS - 1)], 5)
    dep_copy.wait()

    pltpu.make_async_copy(a2_recv, a2_recv, recv_sem.at[6]).wait()
    gathered = a2_recv[...].reshape(LAT, 128)
    smooth = lax.dot_general(
        gathered, kern_v[...], (((0,), (0,)), ((), ())), preferred_element_type=F32
    )
    grad_v[...] = smooth[0 : KB * LEV, :] + ctl_v[...].astype(F32)
    grad_copy = pltpu.make_async_copy(grad_v, grad_hbm, out_sem.at[1])
    grad_copy.start()
    sent(a2_send.at[pl.ds(0, MP - 1)], 6)
    grad_copy.wait()


def shards(
    ensemble, control, band, wind_east, wind_north, observation_longitude, innovation,
    observation_weight,
):
    operands = (
        ensemble.reshape(TILE * LEV, LON),
        jnp.transpose(control, (1, 3, 2, 0)).reshape(KB * LEV, LAT),
        band.reshape(1, LAT),
        wind_east.reshape(TILE * LEV, LON),
        wind_north.reshape(TILE * LEV, LON),
        observation_longitude,
        innovation.reshape(SLOTS * TILE * LEV, OBS),
        observation_weight,
    )
    anywhere = pl.BlockSpec(memory_space=pl.ANY)
    outs = (
        jax.ShapeDtypeStruct((KB * LEV, LAT), F32),
        jax.ShapeDtypeStruct((SLOTS * TILE, OBS), F32),
    )
    scratch = [pltpu.VMEM(x.shape, x.dtype) for x in operands]
    scratch += [pltpu.VMEM(x.shape, x.dtype) for x in outs]
    scratch += [
        pltpu.VMEM((LAT, LAT), BF16),
        pltpu.VMEM((LAT, 128), F32),
        pltpu.VMEM((WIDE, 128), F32),
        pltpu.VMEM((TILE * LEV, WIDE), F32),
        pltpu.VMEM((SLOTS, ROWS, WIDE), F32),
        pltpu.VMEM((MP, 8, 128), BF16),
        pltpu.VMEM((MP, 8, 128), BF16),
        pltpu.VMEM((LEV * 16, 128), F32),
        pltpu.VMEM((ENS - 1, 16, 128), F32),
        pltpu.VMEM((16, 128), F32),
        pltpu.VMEM((4, 16, 128), F32),
        pltpu.VMEM((8, WIDE), F32),
        pltpu.VMEM((4, 8, WIDE), F32),
        pltpu.VMEM((32, WIDE), F32),
        pltpu.VMEM((2, 32, WIDE), F32),
        pltpu.VMEM((5, ROWS, WIDE), F32),
        pltpu.VMEM((SLOTS, ROWS, WIDE), F32),
        pltpu.VMEM((SLOTS, ROWS, WIDE), F32),
        pltpu.VMEM((16, 128), F32),
        pltpu.VMEM((ENS, 16, 128), F32),
        pltpu.VMEM((MP, TILE, 128), BF16),
        pltpu.VMEM((MP, TILE, 128), BF16),
        pltpu.SemaphoreType.DMA((8,)),
        pltpu.SemaphoreType.DMA((2,)),
        pltpu.SemaphoreType.DMA((7,)),
        pltpu.SemaphoreType.DMA((7,)),
    ]
    gradient, departures = pl.pallas_call(
        body,
        out_shape=outs,
        in_specs=[anywhere] * len(operands),
        out_specs=(anywhere, anywhere),
        scratch_shapes=scratch,
        compiler_params=pltpu.CompilerParams(collective_id=0, has_side_effects=True),
        name="assimilate",
    )(*operands)
    gradient = jnp.transpose(gradient.reshape(1, KB, LEV, LAT), (3, 0, 2, 1))
    return gradient, departures.reshape(SLOTS, TILE, 1, OBS)


def solution(mesh):
    placed = (
        P("mp", "ens", None, None),
        P(None, "ens", None, "mp"),
        P(),
        P("mp", None, None),
        P("mp", None, None),
        P(None, "mp", None),
        P(None, "mp", None, None),
        P(None, "mp", None),
    )
    return jax.shard_map(
        shards,
        mesh=mesh,
        in_specs=placed,
        out_specs=(P(None, "ens", None, "mp"), P(None, "mp", "ens", None)),
        check_vma=False,
    )
```

time: 157 us -> 58.2 us (0.37)
  waiting for transfers between devices: 56.1 us -> 0 us
  Pallas kernels: 0 us -> 55.3 us
  starting transfers between devices: 47.7 us -> 0 us
  blocking collectives: 32.9 us -> 0 us
  local copies, waits for them, and re-layouts: 10.5 us -> 2.15 us
  matrix products: 6.36 us -> 0 us
  other arithmetic: 2.16 us -> 0 us
    pallas_call x0 -> x1, Pallas kernels: none -> 55.3 us  [shards(): pl.pallas_call(body, out_shape=outs, in_specs=[anywhere] * len(operands),...]
    all_to_all x2 -> x0, waiting for transfers between devices: 49.9 us -> none  [the longest x1 38.5 us: from_everyone(): lax.all_to_all(jnp.broadcast_to(array[None], (count, *array.shape)), axis...]
    all_to_all x2 -> x0, starting transfers between devices: 35.6 us -> none  [the longest x1 28.4 us: shards(): lax.all_to_all(product, 'mp', split_axis=3, concat_axis=0, tiled=True)]
    all_to_all x1 -> x0, blocking collectives: 32.9 us -> none  [shards(): lax.all_to_all(spread, 'mp', split_axis=0, concat_axis=3, tiled=True)]
    ppermute x4 -> x0, starting transfers between devices: 12.1 us -> none  [the longest x2 6.86 us: padded(): lax.ppermute(lax.slice_in_dim(block, block.shape[dim] - width, None, axis...]
    dot_general x10 -> x0, matrix products: 6.36 us -> none  [the longest x4 3.85 us: inject(): jnp.einsum('ilo,iok->ilk', amounts, picks, precision=lax.Precision.HIGHEST)]
    ppermute x4 -> x0, waiting for transfers between devices: 6.22 us -> none  [the longest x2 3.86 us: padded(): lax.ppermute(lax.slice_in_dim(block, 0, width, axis=dim), axis, backward)]
    slice x25 -> x0, local copies, waits for them, and re-layouts: 1.93 us -> none  [the longest x8 0.88 us: forward_local(): jnp.roll(quantity, -1, axis=2)]
  transfers between devices with their start and end apart: 6 -> 0, of which waited for: 6 -> 0; matrix products, arithmetic and copies ran while one was open for 0% -> 0% of each run, Pallas kernels for 0% -> 0%
where the time goes in v1:
time: 58.2 us; the launch traced here: 58.1 us
  Pallas kernels  55.3 us (95%)
  local copies, waits for them, and re-layouts  2.15 us (4%)
  between operations  0.65 us (1%)
    pallas_call x1, Pallas kernels, shards(): pl.pallas_call(body, out_shape=outs, in_specs=[anywhere] * len(operands),...  55.3 us
    unnamed x4, local copies, waits for them, and re-layouts  2.15 us

profile of v1, /device:TPU:1, one launch (start us, length us, event | category | flops | bytes accessed | tf_op | source)
XLA Modules:
  0.0 58.1 jit_solution(5660794198094370582)
XLA Ops:
  0.6 55.3 %assimilate.1 = (f32[96,192]{1,0:T(8,128)}, f32[16,128]{1,0:T(8,128)}) custom-call(bf16[64,288]{1,0:T(8,128)(2,1)} %bitcast.16, bf16[96,192]{1,0:T(8,128)(2,1)} %bitcast.17, s32[1,192]{1,0:T(1,128)} %bitcast.21, bf16[64,288]{1,0:T(8,128)(2,1)} %bitcast.18, bf16[64,288]{1,0:T(8,128)(2,1)} %bitcast.19, s32[4,4,128]{2,1,0:T(4,128)} %lon_hbm.1, ...), custom_call_target="tpu_custom_call" | custom-call | tf_op jit(solution)/shard_map/assimilate/pallas_call | solution.py:391
  55.9 0.0 copy-start
  55.9 1.5 %copy.13 = f32[192,1,16,6]{0,2,3,1:T(8,128)} copy(f32[192,1,16,6]{0,2,3,1:T(8,128)} %bitcast.15) | data formatting | bytes 147456
  57.5 0.0 copy-done
  57.5 0.6 %copy.14 = f32[4,4,1,128]{3,2,1,0:T(1,128)} copy(f32[4,4,1,128]{3,2,1,0:T(1,128)S(1)} %bitcast.20) | data formatting | bytes 16384
Async XLA Ops:
  55.9 1.6 %copy-start = (f32[16,128]{1,0:T(8,128)S(1)}, f32[16,128]{1,0:T(8,128)}, u32[]{:S(2)}) copy-start(f32[16,128]{1,0:T(8,128)} %get-tuple-element.5) | copy-start | bytes 24580

commit v2 on v1

v2 whole, which is shorter than its diff:
```python
import jax
import jax.numpy as jnp
from jax import lax
from jax.experimental import pallas as pl
from jax.experimental.pallas import tpu as pltpu
from jax.sharding import PartitionSpec as P

MESH = pl.DeviceIdType.MESH
MP, ENS = 48, 16
LAT, LEV, LON, OBS, SLOTS = 192, 16, 288, 128, 4
TILE = 4
KB = 6
WIDE = MP * 8
LATP = 256
KROWS = 24
FIELDS = 80
F32, BF16 = jnp.float32, jnp.bfloat16


def iota(shape, dim):
    return lax.broadcasted_iota(jnp.int32, shape, dim)


def split3(value):
    first = value.astype(BF16)
    rest = value - first.astype(F32)
    second = rest.astype(BF16)
    third = (rest - second.astype(F32)).astype(BF16)
    return first.astype(F32), second.astype(F32), third.astype(F32)


def body(
    ens_hbm, ctl_hbm, band_hbm, east_hbm, north_hbm, lon_hbm, inn_hbm, wgt_hbm,
    grad_hbm, dep_hbm,
    ens_v, ctl_v, band_v, east_v, north_v, lon_v, inn_v, wgt_v, grad_v, dep_v,
    kern_v, rows_v, wide_v, spread_v, ensk_v, embed_v,
    a1_send, a1_recv, sparse_v, f_send, f_recv, fld_v, fld_near, fld_far,
    part_v, rs_recv, inc_v, halo_recv, state_v, coef_v, dfull_v, bfull_v,
    parts_v, s_send, s_recv, ag_send, ag_recv, samp_v,
    in_sem, out_sem, send_sem, recv_sem,
):
    q = lax.axis_index("mp")
    e = lax.axis_index("ens")

    barrier = pltpu.get_barrier_semaphore()

    def greet_mp(d, carry):
        pl.semaphore_signal(
            barrier, inc=1, device_id={"mp": (q + d) % MP}, device_id_type=MESH
        )
        return carry

    def greet_ens(d, carry):
        pl.semaphore_signal(
            barrier, inc=1, device_id={"ens": (e + d) % ENS}, device_id_type=MESH
        )
        return carry

    lax.fori_loop(1, MP, greet_mp, 0)
    lax.fori_loop(1, ENS, greet_ens, 0)
    pairs = [
        (ens_hbm, ens_v), (ctl_hbm, ctl_v), (band_hbm, band_v), (east_hbm, east_v),
        (north_hbm, north_v), (lon_hbm, lon_v), (inn_hbm, inn_v), (wgt_hbm, wgt_v),
    ]
    loads = [
        pltpu.make_async_copy(src, dst, in_sem.at[n]) for n, (src, dst) in enumerate(pairs)
    ]
    for copy in loads:
        copy.start()

    for ref in (sparse_v, fld_v, part_v, ag_send, state_v, dfull_v, bfull_v, parts_v):
        ref[...] = jnp.zeros_like(ref)

    source = iota((LON, WIDE), 1)
    embed_v[...] = (
        (iota((LON, WIDE), 0) == (source >> 3) * 6 + (source & 7)) & ((source & 7) < KB)
    ).astype(F32).astype(BF16)
    group = iota((MP, 128), 1) >> 4
    loads[0].wait()
    padded = jnp.dot(ens_v[...], embed_v[...], preferred_element_type=F32)
    wide_v[...] = jnp.concatenate([padded, jnp.zeros((128 - TILE * LEV, WIDE), F32)], axis=0).T
    by_lon = [wide_v[pl.ds(k, MP, stride=8), :] for k in range(KB)]
    for i in range(TILE):
        block = jnp.zeros((MP, 128), F32)
        for k in range(KB):
            block = jnp.where(group == k, pltpu.roll(by_lon[k], (16 * (k - i)) % 128, 1), block)
        rows_v[pl.ds(i, MP, stride=TILE), :] = block
    a1_send[...] = rows_v[...].reshape(MP, TILE, 128).astype(BF16)

    pl.semaphore_wait(barrier, MP + ENS - 2)

    def to_blocks(src, dst, n):
        def send(d, carry):
            to = (q + d) % MP
            pltpu.make_async_remote_copy(
                src_ref=src.at[to], dst_ref=dst.at[q],
                send_sem=send_sem.at[n], recv_sem=recv_sem.at[n],
                device_id={"mp": to}, device_id_type=MESH,
            ).start()
            return carry

        lax.fori_loop(1, MP, send, 0)
        pltpu.make_async_copy(src.at[q], dst.at[q], recv_sem.at[n]).start()

    def to_near(src, dst, slots, n):
        for slot, offset in slots:
            pltpu.make_async_remote_copy(
                src_ref=src, dst_ref=dst.at[slot], send_sem=send_sem.at[n],
                recv_sem=recv_sem.at[n],
                device_id={"mp": (q - offset + MP) % MP}, device_id_type=MESH,
            ).start()

    def arrived(ref, n):
        pltpu.make_async_copy(ref, ref, recv_sem.at[n]).wait()

    def sent(ref, n):
        pltpu.make_async_copy(ref, ref, send_sem.at[n]).wait()

    to_blocks(a1_send, a1_recv, 0)

    for copy in loads[3:]:
        copy.wait()
    mine = iota((LEV, LON), 0) == e
    winds = []
    for ref in (east_v, north_v):
        for i in range(TILE):
            level = ref[LEV * i : LEV * (i + 1), :].astype(F32)
            winds.append(jnp.sum(jnp.where(mine, level, 0.0), axis=0, keepdims=True))
    wide_winds = jnp.dot(
        jnp.concatenate(winds, axis=0).astype(BF16), embed_v[...], preferred_element_type=F32
    )
    for i in range(TILE):
        sparse_v[i, 64:65, :] = wide_winds[i : i + 1]
        sparse_v[i, 72:73, :] = wide_winds[TILE + i : TILE + i + 1]
    own_level = iota((LEV, OBS), 0) == e
    lane_rows = iota((WIDE, OBS), 0)
    blocks, inner, observed = [], [], []
    for t in range(SLOTS):
        lon = lon_v[t]
        block = (lon * 10923) >> 16
        place = lon + 2 * block
        blocks.append(block)
        inner.append(lon - 6 * block)
        weight = wgt_v[t]
        level_rows = []
        for i in range(TILE):
            start = LEV * (TILE * t + i)
            level_rows.append(
                jnp.sum(
                    jnp.where(own_level, inn_v[start : start + LEV, :], 0.0),
                    axis=0, keepdims=True,
                )
            )
        level_innovation = jnp.concatenate(level_rows, axis=0)
        observed.append(level_innovation)
        parts = split3(weight) + split3(weight * level_innovation)
        for i in range(TILE):
            hits = (lane_rows == place[i : i + 1, :]).astype(F32).astype(BF16)
            lhs = jnp.concatenate(
                [part[i : i + 1, :] for part in parts] + [jnp.zeros((2, OBS), F32)], axis=0
            ).astype(BF16)
            sums = lax.dot_general(
                lhs, hits, (((1,), (1,)), ((), ())), preferred_element_type=F32
            )
            sparse_v[i, 8 * t : 8 * t + 1, :] = sums[0:1] + sums[1:2] + sums[2:3]
            sparse_v[i, 32 + 8 * t : 33 + 8 * t, :] = sums[3:4] + sums[4:5] + sums[5:6]
    for i in range(TILE):
        wide_v[...] = sparse_v[i].T
        spaced = wide_v[pl.ds(0, MP, stride=8), :]
        for k in range(1, KB):
            spaced = spaced + pltpu.roll(wide_v[pl.ds(k, MP, stride=8), :], k, 1)
        rows_v[pl.ds(i, MP, stride=TILE), :] = spaced
    f_send[...] = rows_v[...].reshape(MP, TILE, 128)
    to_blocks(f_send, f_recv, 1)

    for copy in loads[1:3]:
        copy.wait()
    band = jnp.concatenate([band_v[...].astype(F32), jnp.ones((1, LATP - LAT), F32)], axis=1)
    width_j = jnp.broadcast_to(band, (LATP, LATP))
    width_i = width_j.T
    row, column = iota((LATP, LATP), 0), iota((LATP, LATP), 1)
    distance = jnp.abs(row - column).astype(F32)
    weights = jnp.maximum(0.0, 1.0 - 2.0 * distance / (width_i + width_j))
    kern_v[...] = jnp.where((row < LAT) & (column < LAT), weights, 0.0).astype(BF16)
    spread = jnp.dot(ctl_v[...], kern_v[0:LAT, :], preferred_element_type=F32)
    spread_v[...] = spread.astype(BF16).astype(F32)

    arrived(a1_recv, 0)
    gathered = a1_recv[...].astype(F32).reshape(LAT, 128)
    ensk = jnp.concatenate([gathered, jnp.zeros((LATP - LAT, 128), F32)], axis=0).T
    ensk_v[...] = ensk[0 : KB * LEV, :]
    part = ensk[0 : KB * LEV, :] * spread_v[...]
    for k in range(KB):
        for h in range(2):
            part_v[pl.ds(8 * h + k, LEV, stride=16), :] = part[
                LEV * k : LEV * (k + 1), 128 * h : 128 * (h + 1)
            ]

    def send_part(d, carry):
        to = (e + d) % ENS
        pltpu.make_async_remote_copy(
            src_ref=part_v.at[pl.ds(pl.multiple_of(to * 16, 16), 16)], dst_ref=rs_recv.at[d - 1],
            send_sem=send_sem.at[4], recv_sem=recv_sem.at[4],
            device_id={"ens": to}, device_id_type=MESH,
        ).start()
        return carry

    lax.fori_loop(1, ENS, send_part, 0)

    arrived(f_recv, 1)
    fields = f_recv[...].reshape(LAT, 128)
    fields = jnp.concatenate([fields, jnp.zeros((LATP - LAT, 128), F32)], axis=0).T
    fld_v[...] = fields[0:FIELDS, :]
    to_near(fld_v, fld_near, ((0, -1), (1, 1)), 2)
    to_near(fld_v.at[pl.ds(64, 16)], fld_far, ((0, -2), (1, 2)), 3)
    arrived(fld_near, 2)
    arrived(fld_far, 3)
    inside = (iota((KROWS, LATP), 1) < LAT) & (iota((KROWS, LATP), 0) < 22)
    blank = jnp.zeros((2, LATP), F32)
    winds = []
    for at in (0, 8):
        winds.append(
            jnp.concatenate(
                [
                    fld_far[0, at + 4 : at + 6, :], fld_near[0, 64 + at : 70 + at, :],
                    fld_v[64 + at : 70 + at, :], fld_near[1, 64 + at : 70 + at, :],
                    fld_far[1, at : at + 2, :], blank,
                ],
                axis=0,
            )
        )
    east, north = winds
    coefs = (
        1.0 - jnp.abs(east) - jnp.abs(north),
        jnp.maximum(east, 0.0), jnp.maximum(-east, 0.0),
        jnp.maximum(north, 0.0), jnp.maximum(-north, 0.0),
    )
    for n, coef in enumerate(coefs):
        coef_v[n] = jnp.where(inside, coef, 0.0)
    for t in range(SLOTS):
        for full, base in ((dfull_v, 8 * t), (bfull_v, 32 + 8 * t)):
            full[t, 2:8, :] = fld_near[0, base : base + 6, :]
            full[t, 8:14, :] = fld_v[base : base + 6, :]
            full[t, 14:20, :] = fld_near[1, base : base + 6, :]

    own_part = part_v[pl.ds(pl.multiple_of(e * 16, 16), 16), :]
    arrived(rs_recv, 4)
    total = own_part
    for d in range(ENS - 1):
        total = total + rs_recv[d]
    inc_v[:, 0:128] = total[0:8]
    inc_v[:, 128:256] = total[8:16]
    to_near(inc_v, halo_recv, ((0, -2), (1, -1), (2, 1), (3, 2)), 5)
    arrived(halo_recv, 5)
    state_v[0, 0:2, :] = halo_recv[0, 4:6, :]
    state_v[0, 2:8, :] = halo_recv[1, 0:6, :]
    state_v[0, 8:14, :] = inc_v[0:6, :]
    state_v[0, 14:20, :] = halo_recv[2, 0:6, :]
    state_v[0, 20:22, :] = halo_recv[3, 0:2, :]

    def west(value):
        return pltpu.roll(value, 1, 0)

    def east_of(value):
        return pltpu.roll(value, KROWS - 1, 0)

    def below(value):
        return pltpu.roll(value, 1, 1)

    def above(value):
        return pltpu.roll(value, LATP - 1, 1)

    center, from_west, from_east, from_south, from_north = [coef_v[n] for n in range(5)]
    quantity = state_v[0]
    for t in range(SLOTS):
        quantity = (
            center * quantity + from_west * west(quantity) + from_east * east_of(quantity)
            + from_south * below(quantity) + from_north * above(quantity)
        )
        state_v[t] = quantity
        for n, piece in enumerate(split3(quantity[8:14, :])):
            parts_v[32 * n + 8 * t : 32 * n + 8 * t + 6, :] = piece

    s_send[...] = parts_v[...].T[0:LAT, :].reshape(MP, TILE, 128).astype(BF16)
    to_blocks(s_send, s_recv, 6)

    sens = jnp.zeros((KROWS, LATP), F32)
    for t in reversed(range(SLOTS)):
        sens = sens + (dfull_v[t] * state_v[t] - bfull_v[t])
        sens = (
            center * sens + east_of(from_west * sens) + west(from_east * sens)
            + above(from_south * sens) + below(from_north * sens)
        )
    ag_send[0:KB, :] = sens[8:14, :]

    def send_level(d, carry):
        pltpu.make_async_remote_copy(
            src_ref=ag_send, dst_ref=ag_recv.at[e],
            send_sem=send_sem.at[7], recv_sem=recv_sem.at[7],
            device_id={"ens": (e + d) % ENS}, device_id_type=MESH,
        ).start()
        return carry

    lax.fori_loop(1, ENS, send_level, 0)
    pltpu.make_async_copy(ag_send, ag_recv.at[e], recv_sem.at[7]).start()

    sent(a1_send.at[pl.ds(0, MP - 1)], 0)
    sent(f_send.at[pl.ds(0, MP - 1)], 1)
    sent(fld_near, 2)
    sent(fld_far, 3)
    sent(rs_recv, 4)
    sent(halo_recv, 5)

    arrived(ag_recv, 7)
    products = jnp.concatenate(
        [
            (ensk_v[LEV * k : LEV * (k + 1), :] * ag_recv[:, k, :]).astype(BF16).astype(F32)
            for k in range(KB)
        ],
        axis=0,
    ).astype(BF16)
    smooth = jnp.dot(products, kern_v[...], preferred_element_type=F32)
    grad_v[...] = smooth[:, 0:LAT] + ctl_v[...].astype(F32)
    grad_copy = pltpu.make_async_copy(grad_v, grad_hbm, out_sem.at[1])
    grad_copy.start()

    arrived(s_recv, 6)
    states = s_recv[...].astype(F32).reshape(LAT, 128)
    states = jnp.concatenate([states, jnp.zeros((LATP - LAT, 128), F32)], axis=0).T
    samp_v[...] = states[0:32, :] + states[32:64, :] + states[64:96, :]
    tile_row = iota((8, OBS), 0) & 3
    for h in range(2):
        block = jnp.concatenate(blocks[2 * h : 2 * h + 2], axis=0)
        lon_in = jnp.concatenate(inner[2 * h : 2 * h + 2], axis=0)
        index = TILE * block + tile_row
        within, half = index & 127, index >> 7
        sampled = jnp.zeros((8, OBS), F32)
        for k in range(KB):
            at = 16 * h + k
            both = jnp.concatenate(
                [
                    jnp.broadcast_to(samp_v[at : at + 1, :], (TILE, LATP)),
                    jnp.broadcast_to(samp_v[at + 8 : at + 9, :], (TILE, LATP)),
                ],
                axis=0,
            )
            low = jnp.take_along_axis(both[:, 0:128], within, axis=1)
            high = jnp.take_along_axis(both[:, 128:256], within, axis=1)
            sampled = jnp.where(lon_in == k, jnp.where(half == 0, low, high), sampled)
        dep_v[8 * h : 8 * h + 8, :] = sampled - jnp.concatenate(observed[2 * h : 2 * h + 2], axis=0)
    dep_copy = pltpu.make_async_copy(dep_v, dep_hbm, out_sem.at[0])
    dep_copy.start()
    sent(s_send.at[pl.ds(0, MP - 1)], 6)
    sent(ag_recv.at[pl.ds(0, ENS - 1)], 7)
    dep_copy.wait()
    grad_copy.wait()


def shards(
    ensemble, control, band, wind_east, wind_north, observation_longitude, innovation,
    observation_weight,
):
    operands = (
        ensemble.reshape(TILE * LEV, LON),
        jnp.transpose(control, (1, 3, 2, 0)).reshape(KB * LEV, LAT),
        band.reshape(1, LAT),
        wind_east.reshape(TILE * LEV, LON),
        wind_north.reshape(TILE * LEV, LON),
        observation_longitude,
        innovation.reshape(SLOTS * TILE * LEV, OBS),
        observation_weight,
    )
    operands = tuple(pltpu.with_memory_space_constraint(x, pltpu.HBM) for x in operands)
    anywhere = pl.BlockSpec(memory_space=pl.ANY)
    outs = (
        jax.ShapeDtypeStruct((KB * LEV, LAT), F32),
        jax.ShapeDtypeStruct((SLOTS * TILE, OBS), F32),
    )
    scratch = [pltpu.VMEM(x.shape, x.dtype) for x in operands]
    scratch += [pltpu.VMEM(x.shape, x.dtype) for x in outs]
    scratch += [
        pltpu.VMEM((LATP, LATP), BF16),
        pltpu.VMEM((LAT, 128), F32),
        pltpu.VMEM((WIDE, 128), F32),
        pltpu.VMEM((KB * LEV, LATP), F32),
        pltpu.VMEM((KB * LEV, LATP), F32),
        pltpu.VMEM((LON, WIDE), BF16),
        pltpu.VMEM((MP, TILE, 128), BF16),
        pltpu.VMEM((MP, TILE, 128), BF16),
        pltpu.VMEM((TILE, 128, WIDE), F32),
        pltpu.VMEM((MP, TILE, 128), F32),
        pltpu.VMEM((MP, TILE, 128), F32),
        pltpu.VMEM((FIELDS, LATP), F32),
        pltpu.VMEM((2, FIELDS, LATP), F32),
        pltpu.VMEM((2, 16, LATP), F32),
        pltpu.VMEM((LEV * 16, 128), F32),
        pltpu.VMEM((ENS - 1, 16, 128), F32),
        pltpu.VMEM((8, LATP), F32),
        pltpu.VMEM((4, 8, LATP), F32),
        pltpu.VMEM((SLOTS, KROWS, LATP), F32),
        pltpu.VMEM((5, KROWS, LATP), F32),
        pltpu.VMEM((SLOTS, KROWS, LATP), F32),
        pltpu.VMEM((SLOTS, KROWS, LATP), F32),
        pltpu.VMEM((128, LATP), F32),
        pltpu.VMEM((MP, TILE, 128), BF16),
        pltpu.VMEM((MP, TILE, 128), BF16),
        pltpu.VMEM((8, LATP), F32),
        pltpu.VMEM((ENS, 8, LATP), F32),
        pltpu.VMEM((32, LATP), F32),
        pltpu.SemaphoreType.DMA((8,)),
        pltpu.SemaphoreType.DMA((2,)),
        pltpu.SemaphoreType.DMA((8,)),
        pltpu.SemaphoreType.DMA((8,)),
    ]
    gradient, departures = pl.pallas_call(
        body,
        out_shape=outs,
        in_specs=[anywhere] * len(operands),
        out_specs=(anywhere, anywhere),
        scratch_shapes=scratch,
        compiler_params=pltpu.CompilerParams(
            collective_id=0, has_side_effects=True, vmem_limit_bytes=16 * 1024 * 1024
        ),
        name="assimilate",
    )(*operands)
    gradient = jnp.transpose(gradient.reshape(1, KB, LEV, LAT), (3, 0, 2, 1))
    return gradient, departures.reshape(SLOTS, TILE, 1, OBS)


def solution(mesh):
    placed = (
        P("mp", "ens", None, None),
        P(None, "ens", None, "mp"),
        P(),
        P("mp", None, None),
        P("mp", None, None),
        P(None, "mp", None),
        P(None, "mp", None, None),
        P(None, "mp", None),
    )
    return jax.shard_map(
        shards,
        mesh=mesh,
        in_specs=placed,
        out_specs=(P(None, "ens", None, "mp"), P(None, "mp", "ens", None)),
        check_vma=False,
    )
```

time: 58.2 us -> 54.5 us (0.936)
  Pallas kernels: 55.3 us -> 52.5 us
  local copies, waits for them, and re-layouts: 2.15 us -> 1.24 us
    pallas_call x1, Pallas kernels: 55.3 us -> 52.5 us  [shards(): pl.pallas_call(body, out_shape=outs, in_specs=[anywhere] * len(operands),...]
    unnamed x4 -> x2, local copies, waits for them, and re-layouts: 2.15 us -> 1.24 us
where the time goes in v2:
time: 54.5 us; the launch traced here: 54.4 us
  Pallas kernels  52.5 us (96%)
  local copies, waits for them, and re-layouts  1.24 us (2%)
  between operations  0.64 us (1%)
    pallas_call x1, Pallas kernels, shards(): pl.pallas_call(body, out_shape=outs, in_specs=[anywhere] * len(operands),...  52.5 us
    unnamed x2, local copies, waits for them, and re-layouts  1.24 us

profile of v2, /device:TPU:1, one launch (start us, length us, event | category | flops | bytes accessed | tf_op | source)
XLA Modules:
  0.0 54.4 jit_solution(1844705957505188552)
XLA Ops:
  0.6 52.5 %assimilate.1 = (f32[96,192]{1,0:T(8,128)S(1)}, f32[16,128]{1,0:T(8,128)S(1)}) custom-call(bf16[64,288]{1,0:T(8,128)(2,1)} %bitcast.17, bf16[96,192]{1,0:T(8,128)(2,1)} %bitcast.18, s32[1,192]{1,0:T(1,128)} %bitcast.21, bf16[64,288]{1,0:T(8,128)(2,1)} %bitcast.19, bf16[64,288]{1,0:T(8,128)(2,1)} %bitcast.20, s32[4,4,128]{2,1,0:T(4,128)} %lon_hbm.1, ...), custom_call_target="tpu_custom_call" | custom-call | tf_op jit(solution)/shard_map/assimilate/pallas_call | solution.py:415
  53.2 0.6 %copy.13 = f32[192,1,16,6]{0,2,3,1:T(8,128)} copy(f32[192,1,16,6]{0,2,3,1:T(8,128)S(1)} %bitcast.14) | data formatting | bytes 147456
  53.8 0.6 %copy.14 = f32[4,4,1,128]{3,2,1,0:T(1,128)} copy(f32[4,4,1,128]{3,2,1,0:T(1,128)S(1)} %bitcast.15) | data formatting | bytes 16384

commit v3 on v2

--- a/solution.py
+++ b/solution.py
@@ -7,7 +7,12 @@
 
 MESH = pl.DeviceIdType.MESH
 MP, ENS = 48, 16
+PLANES, PLANE = 3, 16
 LAT, LEV, LON, OBS, SLOTS = 192, 16, 288, 128, 4
+FARTHEST = sorted(
+    [(z, y, c) for z in range(PLANES) for y in range(8) for c in range(2) if z or y or c],
+    key=lambda d: (-4 * (d[0] > 0) - min(d[1], 8 - d[1]), d),
+)
 TILE = 4
 KB = 6
 WIDE = MP * 8
@@ -31,22 +36,30 @@
 
 def body(
     ens_hbm, ctl_hbm, band_hbm, east_hbm, north_hbm, lon_hbm, inn_hbm, wgt_hbm,
-    grad_hbm, dep_hbm,
-    ens_v, ctl_v, band_v, east_v, north_v, lon_v, inn_v, wgt_v, grad_v, dep_v,
+    grad_v, dep_v,
+    ens_v, ctl_v, band_v, east_v, north_v, lon_v, inn_v, wgt_v,
     kern_v, rows_v, wide_v, spread_v, ensk_v, embed_v,
-    a1_send, a1_recv, sparse_v, f_send, f_recv, fld_v, fld_near, fld_far,
+    a1_send, a1_mid, a1_recv, sparse_v, f_send, f_mid, f_recv, fld_v, fld_near, fld_far,
     part_v, rs_recv, inc_v, halo_recv, state_v, coef_v, dfull_v, bfull_v,
     parts_v, s_send, s_recv, ag_send, ag_recv, samp_v,
-    in_sem, out_sem, send_sem, recv_sem,
+    in_sem, send_sem, recv_sem,
 ):
     q = lax.axis_index("mp")
     e = lax.axis_index("ens")
+    plane, rank = q // PLANE, q % PLANE
 
     barrier = pltpu.get_barrier_semaphore()
 
-    def greet_mp(d, carry):
+    def greet_plane(d, carry):
         pl.semaphore_signal(
-            barrier, inc=1, device_id={"mp": (q + d) % MP}, device_id_type=MESH
+            barrier, inc=1, device_id={"mp": plane * PLANE + (rank + d) % PLANE},
+            device_id_type=MESH,
+        )
+        return carry
+
+    def greet_line(d, carry):
+        pl.semaphore_signal(
+            barrier, inc=1, device_id={"mp": (q + PLANE * d) % MP}, device_id_type=MESH
         )
         return carry
 
@@ -56,8 +69,9 @@
         )
         return carry
 
-    lax.fori_loop(1, MP, greet_mp, 0)
     lax.fori_loop(1, ENS, greet_ens, 0)
+    lax.fori_loop(1, PLANES, greet_line, 0)
+    lax.fori_loop(1, PLANE, greet_plane, 0)
     pairs = [
         (ens_hbm, ens_v), (ctl_hbm, ctl_v), (band_hbm, band_v), (east_hbm, east_v),
         (north_hbm, north_v), (lon_hbm, lon_v), (inn_hbm, inn_v), (wgt_hbm, wgt_v),
@@ -85,22 +99,43 @@
         for k in range(KB):
             block = jnp.where(group == k, pltpu.roll(by_lon[k], (16 * (k - i)) % 128, 1), block)
         rows_v[pl.ds(i, MP, stride=TILE), :] = block
-    a1_send[...] = rows_v[...].reshape(MP, TILE, 128).astype(BF16)
-
-    pl.semaphore_wait(barrier, MP + ENS - 2)
-
-    def to_blocks(src, dst, n):
+    a1_send[...] = rows_v[...].reshape(PLANES, PLANE, TILE, 128).astype(BF16)
+
+    pl.semaphore_wait(barrier, PLANE + PLANES + ENS - 3)
+
+    def to_plane(src, middle, n):
         def send(d, carry):
-            to = (q + d) % MP
+            to = (rank + d) % PLANE
             pltpu.make_async_remote_copy(
-                src_ref=src.at[to], dst_ref=dst.at[q],
+                src_ref=src.at[:, to], dst_ref=middle.at[rank],
                 send_sem=send_sem.at[n], recv_sem=recv_sem.at[n],
-                device_id={"mp": to}, device_id_type=MESH,
+                device_id={"mp": plane * PLANE + to}, device_id_type=MESH,
             ).start()
             return carry
 
-        lax.fori_loop(1, MP, send, 0)
-        pltpu.make_async_copy(src.at[q], dst.at[q], recv_sem.at[n]).start()
+        lax.fori_loop(1, PLANE, send, 0)
+        pltpu.make_async_copy(src.at[:, rank], middle.at[rank], recv_sem.at[n]).start()
+
+    def to_line(middle, dst, n):
+        for d in range(1, PLANES):
+            to = (plane + d) % PLANES
+            pltpu.make_async_remote_copy(
+                src_ref=middle.at[:, to], dst_ref=dst.at[plane],
+                send_sem=send_sem.at[n], recv_sem=recv_sem.at[n],
+                device_id={"mp": to * PLANE + rank}, device_id_type=MESH,
+            ).start()
+        pltpu.make_async_copy(middle.at[:, plane], dst.at[plane], recv_sem.at[n]).start()
+
+    def to_all(src, dst, n):
+        for dz, dy, dc in FARTHEST:
+            to_z = (plane + dz) % PLANES
+            to_r = (rank // 2 + dy) % 8 * 2 + (rank + dc) % 2
+            pltpu.make_async_remote_copy(
+                src_ref=src.at[to_z, to_r], dst_ref=dst.at[plane, rank],
+                send_sem=send_sem.at[n], recv_sem=recv_sem.at[n],
+                device_id={"mp": to_z * PLANE + to_r}, device_id_type=MESH,
+            ).start()
+        pltpu.make_async_copy(src.at[plane, rank], dst.at[plane, rank], recv_sem.at[n]).start()
 
     def to_near(src, dst, slots, n):
         for slot, offset in slots:
@@ -116,7 +151,7 @@
     def sent(ref, n):
         pltpu.make_async_copy(ref, ref, send_sem.at[n]).wait()
 
-    to_blocks(a1_send, a1_recv, 0)
+    to_plane(a1_send, a1_mid, 0)
 
     for copy in loads[3:]:
         copy.wait()
@@ -170,8 +205,10 @@
         for k in range(1, KB):
             spaced = spaced + pltpu.roll(wide_v[pl.ds(k, MP, stride=8), :], k, 1)
         rows_v[pl.ds(i, MP, stride=TILE), :] = spaced
-    f_send[...] = rows_v[...].reshape(MP, TILE, 128)
-    to_blocks(f_send, f_recv, 1)
+    f_send[...] = rows_v[...].reshape(PLANES, PLANE, TILE, 128)
+    to_plane(f_send, f_mid, 1)
+    arrived(a1_mid, 0)
+    to_line(a1_mid, a1_recv, 8)
 
     for copy in loads[1:3]:
         copy.wait()
@@ -185,7 +222,9 @@
     spread = jnp.dot(ctl_v[...], kern_v[0:LAT, :], preferred_element_type=F32)
     spread_v[...] = spread.astype(BF16).astype(F32)
 
-    arrived(a1_recv, 0)
+    arrived(f_mid, 1)
+    to_line(f_mid, f_recv, 9)
+    arrived(a1_recv, 8)
     gathered = a1_recv[...].astype(F32).reshape(LAT, 128)
     ensk = jnp.concatenate([gathered, jnp.zeros((LATP - LAT, 128), F32)], axis=0).T
     ensk_v[...] = ensk[0 : KB * LEV, :]
@@ -207,12 +246,20 @@
 
     lax.fori_loop(1, ENS, send_part, 0)
 
-    arrived(f_recv, 1)
+    arrived(f_recv, 9)
     fields = f_recv[...].reshape(LAT, 128)
     fields = jnp.concatenate([fields, jnp.zeros((LATP - LAT, 128), F32)], axis=0).T
     fld_v[...] = fields[0:FIELDS, :]
     to_near(fld_v, fld_near, ((0, -1), (1, 1)), 2)
     to_near(fld_v.at[pl.ds(64, 16)], fld_far, ((0, -2), (1, 2)), 3)
+    own_part = part_v[pl.ds(pl.multiple_of(e * 16, 16), 16), :]
+    arrived(rs_recv, 4)
+    total = own_part
+    for d in range(ENS - 1):
+        total = total + rs_recv[d]
+    inc_v[:, 0:128] = total[0:8]
+    inc_v[:, 128:256] = total[8:16]
+    to_near(inc_v, halo_recv, ((0, -2), (1, -1), (2, 1), (3, 2)), 5)
     arrived(fld_near, 2)
     arrived(fld_far, 3)
     inside = (iota((KROWS, LATP), 1) < LAT) & (iota((KROWS, LATP), 0) < 22)
@@ -243,14 +290,6 @@
             full[t, 8:14, :] = fld_v[base : base + 6, :]
             full[t, 14:20, :] = fld_near[1, base : base + 6, :]
 
-    own_part = part_v[pl.ds(pl.multiple_of(e * 16, 16), 16), :]
-    arrived(rs_recv, 4)
-    total = own_part
-    for d in range(ENS - 1):
-        total = total + rs_recv[d]
-    inc_v[:, 0:128] = total[0:8]
-    inc_v[:, 128:256] = total[8:16]
-    to_near(inc_v, halo_recv, ((0, -2), (1, -1), (2, 1), (3, 2)), 5)
     arrived(halo_recv, 5)
     state_v[0, 0:2, :] = halo_recv[0, 4:6, :]
     state_v[0, 2:8, :] = halo_recv[1, 0:6, :]
@@ -281,8 +320,8 @@
         for n, piece in enumerate(split3(quantity[8:14, :])):
             parts_v[32 * n + 8 * t : 32 * n + 8 * t + 6, :] = piece
 
-    s_send[...] = parts_v[...].T[0:LAT, :].reshape(MP, TILE, 128).astype(BF16)
-    to_blocks(s_send, s_recv, 6)
+    s_send[...] = parts_v[...].T[0:LAT, :].reshape(PLANES, PLANE, TILE, 128).astype(BF16)
+    to_all(s_send, s_recv, 6)
 
     sens = jnp.zeros((KROWS, LATP), F32)
     for t in reversed(range(SLOTS)):
@@ -304,8 +343,10 @@
     lax.fori_loop(1, ENS, send_level, 0)
     pltpu.make_async_copy(ag_send, ag_recv.at[e], recv_sem.at[7]).start()
 
-    sent(a1_send.at[pl.ds(0, MP - 1)], 0)
-    sent(f_send.at[pl.ds(0, MP - 1)], 1)
+    sent(a1_mid.at[pl.ds(0, PLANE - 1)], 0)
+    sent(a1_recv.at[pl.ds(0, PLANES - 1)], 8)
+    sent(f_mid.at[pl.ds(0, PLANE - 1)], 1)
+    sent(f_recv.at[pl.ds(0, PLANES - 1)], 9)
     sent(fld_near, 2)
     sent(fld_far, 3)
     sent(rs_recv, 4)
@@ -321,8 +362,6 @@
     ).astype(BF16)
     smooth = jnp.dot(products, kern_v[...], preferred_element_type=F32)
     grad_v[...] = smooth[:, 0:LAT] + ctl_v[...].astype(F32)
-    grad_copy = pltpu.make_async_copy(grad_v, grad_hbm, out_sem.at[1])
-    grad_copy.start()
 
     arrived(s_recv, 6)
     states = s_recv[...].astype(F32).reshape(LAT, 128)
@@ -348,12 +387,21 @@
             high = jnp.take_along_axis(both[:, 128:256], within, axis=1)
             sampled = jnp.where(lon_in == k, jnp.where(half == 0, low, high), sampled)
         dep_v[8 * h : 8 * h + 8, :] = sampled - jnp.concatenate(observed[2 * h : 2 * h + 2], axis=0)
-    dep_copy = pltpu.make_async_copy(dep_v, dep_hbm, out_sem.at[0])
-    dep_copy.start()
-    sent(s_send.at[pl.ds(0, MP - 1)], 6)
+    sent(s_recv.at[0], 6)
+    sent(s_recv.at[1], 6)
+    sent(s_recv.at[2, pl.ds(0, PLANE - 1)], 6)
     sent(ag_recv.at[pl.ds(0, ENS - 1)], 7)
-    dep_copy.wait()
-    grad_copy.wait()
+
+
+def move_out(grad_v, dep_v, grad_hbm, dep_hbm, out_sem):
+    copies = [
+        pltpu.make_async_copy(grad_v, grad_hbm, out_sem.at[0]),
+        pltpu.make_async_copy(dep_v, dep_hbm, out_sem.at[1]),
+    ]
+    for copy in copies:
+        copy.start()
+    for copy in copies:
+        copy.wait()
 
 
 def shards(
@@ -377,7 +425,6 @@
         jax.ShapeDtypeStruct((SLOTS * TILE, OBS), F32),
     )
     scratch = [pltpu.VMEM(x.shape, x.dtype) for x in operands]
-    scratch += [pltpu.VMEM(x.shape, x.dtype) for x in outs]
     scratch += [
         pltpu.VMEM((LATP, LATP), BF16),
         pltpu.VMEM((LAT, 128), F32),
@@ -385,11 +432,13 @@
         pltpu.VMEM((KB * LEV, LATP), F32),
         pltpu.VMEM((KB * LEV, LATP), F32),
         pltpu.VMEM((LON, WIDE), BF16),
-        pltpu.VMEM((MP, TILE, 128), BF16),
-        pltpu.VMEM((MP, TILE, 128), BF16),
+        pltpu.VMEM((PLANES, PLANE, TILE, 128), BF16),
+        pltpu.VMEM((PLANE, PLANES, TILE, 128), BF16),
+        pltpu.VMEM((PLANES, PLANE, TILE, 128), BF16),
         pltpu.VMEM((TILE, 128, WIDE), F32),
-        pltpu.VMEM((MP, TILE, 128), F32),
-        pltpu.VMEM((MP, TILE, 128), F32),
+        pltpu.VMEM((PLANES, PLANE, TILE, 128), F32),
+        pltpu.VMEM((PLANE, PLANES, TILE, 128), F32),
+        pltpu.VMEM((PLANES, PLANE, TILE, 128), F32),
         pltpu.VMEM((FIELDS, LATP), F32),
         pltpu.VMEM((2, FIELDS, LATP), F32),
         pltpu.VMEM((2, 16, LATP), F32),
@@ -402,27 +451,35 @@
         pltpu.VMEM((SLOTS, KROWS, LATP), F32),
         pltpu.VMEM((SLOTS, KROWS, LATP), F32),
         pltpu.VMEM((128, LATP), F32),
-        pltpu.VMEM((MP, TILE, 128), BF16),
-        pltpu.VMEM((MP, TILE, 128), BF16),
+        pltpu.VMEM((PLANES, PLANE, TILE, 128), BF16),
+        pltpu.VMEM((PLANES, PLANE, TILE, 128), BF16),
         pltpu.VMEM((8, LATP), F32),
         pltpu.VMEM((ENS, 8, LATP), F32),
         pltpu.VMEM((32, LATP), F32),
         pltpu.SemaphoreType.DMA((8,)),
-        pltpu.SemaphoreType.DMA((2,)),
-        pltpu.SemaphoreType.DMA((8,)),
-        pltpu.SemaphoreType.DMA((8,)),
+        pltpu.SemaphoreType.DMA((10,)),
+        pltpu.SemaphoreType.DMA((10,)),
     ]
     gradient, departures = pl.pallas_call(
         body,
         out_shape=outs,
         in_specs=[anywhere] * len(operands),
-        out_specs=(anywhere, anywhere),
+        out_specs=(pl.BlockSpec(memory_space=pltpu.VMEM),) * 2,
         scratch_shapes=scratch,
         compiler_params=pltpu.CompilerParams(
             collective_id=0, has_side_effects=True, vmem_limit_bytes=16 * 1024 * 1024
         ),
         name="assimilate",
     )(*operands)
+    gradient, departures = pl.pallas_call(
+        move_out,
+        out_shape=outs,
+        in_specs=[anywhere] * 2,
+        out_specs=(pl.BlockSpec(memory_space=pltpu.HBM),) * 2,
+        scratch_shapes=[pltpu.SemaphoreType.DMA((2,))],
+        compiler_params=pltpu.CompilerParams(vmem_limit_bytes=1024 * 1024),
+        name="move_out",
+    )(gradient, departures)
     gradient = jnp.transpose(gradient.reshape(1, KB, LEV, LAT), (3, 0, 2, 1))
     return gradient, departures.reshape(SLOTS, TILE, 1, OBS)
 

time: 54.5 us -> 52 us (0.954)
  Pallas kernels: 52.5 us -> 51.2 us
  local copies, waits for them, and re-layouts: 1.24 us -> 0 us
    pallas_call x1, Pallas kernels: 52.5 us -> 50.5 us  [shards(): pl.pallas_call(body, out_shape=outs, in_specs=[anywhere] * len(operands),...]
    unnamed x2 -> x0, local copies, waits for them, and re-layouts: 1.24 us -> none
    pallas_call x0 -> x1, Pallas kernels: none -> 0.66 us  [shards(): pl.pallas_call(move_out, out_shape=outs, in_specs=[anywhere] * 2, out_spe...]
where the time goes in v3:
time: 52 us; the launch traced here: 51.8 us
  Pallas kernels  51.2 us (98%)
  between operations  0.64 us (1%)
    pallas_call x1, Pallas kernels, shards(): pl.pallas_call(body, out_shape=outs, in_specs=[anywhere] * len(operands),...  50.5 us

profile of v3, /device:TPU:1, one launch (start us, length us, event | category | flops | bytes accessed | tf_op | source)
XLA Modules:
  0.0 51.8 jit_solution(13106930170321821370)
XLA Ops:
  0.6 50.5 %assimilate.1 = (f32[96,192]{1,0:T(8,128)S(1)}, f32[16,128]{1,0:T(8,128)S(1)}) custom-call(bf16[64,288]{1,0:T(8,128)(2,1)} %bitcast.15, bf16[96,192]{1,0:T(8,128)(2,1)} %bitcast.16, s32[1,192]{1,0:T(1,128)} %bitcast.19, bf16[64,288]{1,0:T(8,128)(2,1)} %bitcast.17, bf16[64,288]{1,0:T(8,128)(2,1)} %bitcast.18, s32[4,4,128]{2,1,0:T(4,128)} %lon_hbm.1, ...), custom_call_target="tpu_custom_call" | custom-call | tf_op jit(solution)/shard_map/assimilate/pallas_call | solution.py:463
  51.2 0.7 %move_out.1 = (f32[96,192]{1,0:T(8,128)}, f32[16,128]{1,0:T(8,128)}) custom-call(f32[96,192]{1,0:T(8,128)S(1)} %get-tuple-element.6.grad_v, f32[16,128]{1,0:T(8,128)S(1)} %get-tuple-element.7.dep_v), custom_call_target="tpu_custom_call" | custom-call | tf_op jit(solution)/shard_map/move_out/pallas_call | solution.py:474

commit v4 on v3

--- a/solution.py
+++ b/solution.py
@@ -9,16 +9,16 @@
 MP, ENS = 48, 16
 PLANES, PLANE = 3, 16
 LAT, LEV, LON, OBS, SLOTS = 192, 16, 288, 128, 4
-FARTHEST = sorted(
-    [(z, y, c) for z in range(PLANES) for y in range(8) for c in range(2) if z or y or c],
-    key=lambda d: (-4 * (d[0] > 0) - min(d[1], 8 - d[1]), d),
-)
+LEVEL_ORDER = (8, 9, 7, 10, 6, 11, 5, 12, 4, 13, 3, 14, 2, 15, 1)
 TILE = 4
 KB = 6
 WIDE = MP * 8
 LATP = 256
 KROWS = 24
-FIELDS = 80
+TROWS = 16
+PART, PART2 = jnp.bfloat16, jnp.bfloat16
+SENS = jnp.bfloat16
+FIELDS = 64
 F32, BF16 = jnp.float32, jnp.bfloat16
 
 
@@ -39,9 +39,11 @@
     grad_v, dep_v,
     ens_v, ctl_v, band_v, east_v, north_v, lon_v, inn_v, wgt_v,
     kern_v, rows_v, wide_v, spread_v, ensk_v, embed_v,
-    a1_send, a1_mid, a1_recv, sparse_v, f_send, f_mid, f_recv, fld_v, fld_near, fld_far,
-    part_v, rs_recv, inc_v, halo_recv, state_v, coef_v, dfull_v, bfull_v,
-    parts_v, s_send, s_recv, ag_send, ag_recv, samp_v,
+    a1_send, a1_mid, a1_recv, sparse_v, f_send, f_mid, f_recv, fld_v, fldn_s, fld_near, fldw_v, fldw_s, fldw_recv, pairs_v,
+    part_v, part_s, rs_recv, inc_v, halo_recv, state_v, coef_v, dfull_v, bfull_v,
+    ag_send, ag_recv, level_v,
+    ensw_v, b_send, b_mid, b_recv, part2_v, part2_s, rs2_recv, inc2_v, halo2_recv,
+    wind_v, wind_recv, state2_v, coef2_v,
     in_sem, send_sem, recv_sem,
 ):
     q = lax.axis_index("mp")
@@ -82,7 +84,9 @@
     for copy in loads:
         copy.start()
 
-    for ref in (sparse_v, fld_v, part_v, ag_send, state_v, dfull_v, bfull_v, parts_v):
+    for ref in (
+        sparse_v, fld_v, fldn_s, part_v, state_v, dfull_v, bfull_v, part2_v, state2_v, rows_v
+    ):
         ref[...] = jnp.zeros_like(ref)
 
     source = iota((LON, WIDE), 1)
@@ -92,6 +96,7 @@
     group = iota((MP, 128), 1) >> 4
     loads[0].wait()
     padded = jnp.dot(ens_v[...], embed_v[...], preferred_element_type=F32)
+    ensw_v[...] = padded
     wide_v[...] = jnp.concatenate([padded, jnp.zeros((128 - TILE * LEV, WIDE), F32)], axis=0).T
     by_lon = [wide_v[pl.ds(k, MP, stride=8), :] for k in range(KB)]
     for i in range(TILE):
@@ -126,16 +131,28 @@
             ).start()
         pltpu.make_async_copy(middle.at[:, plane], dst.at[plane], recv_sem.at[n]).start()
 
-    def to_all(src, dst, n):
-        for dz, dy, dc in FARTHEST:
-            to_z = (plane + dz) % PLANES
-            to_r = (rank // 2 + dy) % 8 * 2 + (rank + dc) % 2
+    def line_first(src, middle, n):
+        for d in range(1, PLANES):
+            to = (plane + d) % PLANES
             pltpu.make_async_remote_copy(
-                src_ref=src.at[to_z, to_r], dst_ref=dst.at[plane, rank],
+                src_ref=src.at[to], dst_ref=middle.at[plane],
                 send_sem=send_sem.at[n], recv_sem=recv_sem.at[n],
-                device_id={"mp": to_z * PLANE + to_r}, device_id_type=MESH,
+                device_id={"mp": to * PLANE + rank}, device_id_type=MESH,
             ).start()
-        pltpu.make_async_copy(src.at[plane, rank], dst.at[plane, rank], recv_sem.at[n]).start()
+        pltpu.make_async_copy(src.at[plane], middle.at[plane], recv_sem.at[n]).start()
+
+    def plane_next(middle, dst, n):
+        def send(d, carry):
+            to = (rank + d) % PLANE
+            pltpu.make_async_remote_copy(
+                src_ref=middle.at[:, to], dst_ref=dst.at[:, rank],
+                send_sem=send_sem.at[n], recv_sem=recv_sem.at[n],
+                device_id={"mp": plane * PLANE + to}, device_id_type=MESH,
+            ).start()
+            return carry
+
+        lax.fori_loop(1, PLANE, send, 0)
+        pltpu.make_async_copy(middle.at[:, rank], dst.at[:, rank], recv_sem.at[n]).start()
 
     def to_near(src, dst, slots, n):
         for slot, offset in slots:
@@ -153,7 +170,33 @@
 
     to_plane(a1_send, a1_mid, 0)
 
-    for copy in loads[3:]:
+    for copy in loads[1:3]:
+        copy.wait()
+    band = jnp.concatenate([band_v[...].astype(F32), jnp.ones((1, LATP - LAT), F32)], axis=1)
+    width_j = jnp.broadcast_to(band, (LATP, LATP))
+    width_i = width_j.T
+    row, column = iota((LATP, LATP), 0), iota((LATP, LATP), 1)
+    distance = jnp.abs(row - column).astype(F32)
+    weights = jnp.maximum(0.0, 1.0 - 2.0 * distance / (width_i + width_j))
+    kern_v[...] = jnp.where((row < LAT) & (column < LAT), weights, 0.0).astype(BF16)
+    spread = jnp.dot(ctl_v[...], kern_v[0:LAT, :], preferred_element_type=F32)
+    spread_v[...] = spread.astype(BF16).astype(F32)
+
+
+    by_tile = lax.dot_general(
+        kern_v[0:LAT, 0:LAT], ctl_v[...], (((1,), (1,)), ((), ())), preferred_element_type=F32
+    )
+    rows_v[...] = jnp.concatenate([by_tile, jnp.zeros((LAT, 128 - KB * LEV), F32)], axis=1)
+    by_row = [rows_v[pl.ds(i, MP, stride=TILE), :] for i in range(TILE)]
+    for r in range(TILE - 1):
+        block = jnp.zeros((MP, 128), F32)
+        for h in range(2):
+            k = 2 * r + h
+            for i in range(TILE):
+                moved = pltpu.roll(by_row[i], (64 * h + 16 * (i - k)) % 128, 1)
+                block = jnp.where(group == 4 * h + i, moved, block)
+        rows_v[pl.ds(r, MP, stride=TILE), :] = block
+    for copy in loads[3:5]:
         copy.wait()
     mine = iota((LEV, LON), 0) == e
     winds = []
@@ -164,18 +207,32 @@
     wide_winds = jnp.dot(
         jnp.concatenate(winds, axis=0).astype(BF16), embed_v[...], preferred_element_type=F32
     )
+    wind_v[...] = wide_winds
     for i in range(TILE):
-        sparse_v[i, 64:65, :] = wide_winds[i : i + 1]
-        sparse_v[i, 72:73, :] = wide_winds[TILE + i : TILE + i + 1]
+        sparse_v[0, 16 * i : 16 * i + 1, :] = wide_winds[i : i + 1]
+        sparse_v[0, 16 * i + 8 : 16 * i + 9, :] = wide_winds[TILE + i : TILE + i + 1]
+
+    def spaced(at):
+        wide_v[...] = sparse_v[at].T
+        total = wide_v[pl.ds(0, MP, stride=8), :]
+        for k in range(1, KB):
+            total = total + pltpu.roll(wide_v[pl.ds(k, MP, stride=8), :], k, 1)
+        return total
+
+    rows_v[pl.ds(3, MP, stride=TILE), :] = spaced(0)
+    b_send[...] = rows_v[...].reshape(PLANES, PLANE, TILE, 128).astype(BF16)
+    line_first(b_send, b_mid, 6)
+
+    for copy in loads[5:]:
+        copy.wait()
     own_level = iota((LEV, OBS), 0) == e
     lane_rows = iota((WIDE, OBS), 0)
-    blocks, inner, observed = [], [], []
+    places, observed = [], []
     for t in range(SLOTS):
         lon = lon_v[t]
         block = (lon * 10923) >> 16
         place = lon + 2 * block
-        blocks.append(block)
-        inner.append(lon - 6 * block)
+        places.append(place)
         weight = wgt_v[t]
         level_rows = []
         for i in range(TILE):
@@ -197,33 +254,20 @@
             sums = lax.dot_general(
                 lhs, hits, (((1,), (1,)), ((), ())), preferred_element_type=F32
             )
-            sparse_v[i, 8 * t : 8 * t + 1, :] = sums[0:1] + sums[1:2] + sums[2:3]
-            sparse_v[i, 32 + 8 * t : 33 + 8 * t, :] = sums[3:4] + sums[4:5] + sums[5:6]
-    for i in range(TILE):
-        wide_v[...] = sparse_v[i].T
-        spaced = wide_v[pl.ds(0, MP, stride=8), :]
-        for k in range(1, KB):
-            spaced = spaced + pltpu.roll(wide_v[pl.ds(k, MP, stride=8), :], k, 1)
-        rows_v[pl.ds(i, MP, stride=TILE), :] = spaced
-    f_send[...] = rows_v[...].reshape(PLANES, PLANE, TILE, 128)
-    to_plane(f_send, f_mid, 1)
+            half, to = 1 + i // 2, 64 * (i % 2) + 8 * t
+            sparse_v[half, to : to + 1, :] = sums[0:1] + sums[1:2] + sums[2:3]
+            sparse_v[half, to + 32 : to + 33, :] = sums[3:4] + sums[4:5] + sums[5:6]
+    for half in range(2):
+        pairs_v[pl.ds(half, MP, stride=2), :] = spaced(1 + half)
+    f_send[...] = pairs_v[...].reshape(PLANES, PLANE, 2, 128)
+    line_first(f_send, f_mid, 1)
     arrived(a1_mid, 0)
     to_line(a1_mid, a1_recv, 8)
 
-    for copy in loads[1:3]:
-        copy.wait()
-    band = jnp.concatenate([band_v[...].astype(F32), jnp.ones((1, LATP - LAT), F32)], axis=1)
-    width_j = jnp.broadcast_to(band, (LATP, LATP))
-    width_i = width_j.T
-    row, column = iota((LATP, LATP), 0), iota((LATP, LATP), 1)
-    distance = jnp.abs(row - column).astype(F32)
-    weights = jnp.maximum(0.0, 1.0 - 2.0 * distance / (width_i + width_j))
-    kern_v[...] = jnp.where((row < LAT) & (column < LAT), weights, 0.0).astype(BF16)
-    spread = jnp.dot(ctl_v[...], kern_v[0:LAT, :], preferred_element_type=F32)
-    spread_v[...] = spread.astype(BF16).astype(F32)
-
+    arrived(b_mid, 6)
+    plane_next(b_mid, b_recv, 10)
     arrived(f_mid, 1)
-    to_line(f_mid, f_recv, 9)
+    plane_next(f_mid, f_recv, 9)
     arrived(a1_recv, 8)
     gathered = a1_recv[...].astype(F32).reshape(LAT, 128)
     ensk = jnp.concatenate([gathered, jnp.zeros((LATP - LAT, 128), F32)], axis=0).T
@@ -235,33 +279,72 @@
                 LEV * k : LEV * (k + 1), 128 * h : 128 * (h + 1)
             ]
 
-    def send_part(d, carry):
-        to = (e + d) % ENS
-        pltpu.make_async_remote_copy(
-            src_ref=part_v.at[pl.ds(pl.multiple_of(to * 16, 16), 16)], dst_ref=rs_recv.at[d - 1],
-            send_sem=send_sem.at[4], recv_sem=recv_sem.at[4],
-            device_id={"ens": to}, device_id_type=MESH,
-        ).start()
-        return carry
-
-    lax.fori_loop(1, ENS, send_part, 0)
+    part_s[...] = part_v[...].reshape(LEV, 16, 128).astype(PART)
+
+    def to_levels(src, dst, n):
+        for slot, d in enumerate(LEVEL_ORDER):
+            to = (e + d) % ENS
+            pltpu.make_async_remote_copy(
+                src_ref=src.at[to], dst_ref=dst.at[slot],
+                send_sem=send_sem.at[n], recv_sem=recv_sem.at[n],
+                device_id={"ens": to}, device_id_type=MESH,
+            ).start()
+
+    to_levels(part_s, rs_recv, 4)
+    to_near(wind_v, wind_recv, ((0, -1), (1, 1)), 11)
+
+    arrived(b_recv, 10)
+    rows_v[...] = b_recv[...].astype(F32).reshape(LAT, 128)
+    for r in range(KB // 2):
+        block = rows_v[pl.ds(r, MP, stride=TILE), :]
+        wide_v[pl.ds(2 * r, MP, stride=8), :] = block
+        wide_v[pl.ds(2 * r + 1, MP, stride=8), :] = pltpu.roll(block, 64, 1)
+    native = wide_v[...].T
+    by_block = rows_v[pl.ds(3, MP, stride=TILE), :]
+    for i in range(TILE):
+        rows_v[pl.ds(i, MP, stride=TILE), :] = pltpu.roll(by_block, (-16 * i) % 128, 1)
+    fields = jnp.concatenate([rows_v[...], jnp.zeros((LATP - LAT, 128), F32)], axis=0).T
+    fldw_v[...] = fields[0:16, :]
+    fldw_s[...] = fields[0:16, :].astype(BF16)
+    to_near(fldw_s, fldw_recv, ((0, -2), (1, -1), (2, 1), (3, 2)), 3)
+    for i in range(TILE):
+        own = ensw_v[LEV * i : LEV * (i + 1), :] * native[LEV * i : LEV * (i + 1), :]
+        for c in range(3):
+            part2_v[pl.ds(4 * c + i, LEV, stride=16), :] = own[:, 128 * c : 128 * (c + 1)]
+    part2_s[...] = part2_v[...].reshape(LEV, 16, 128).astype(PART2)
+    to_levels(part2_s, rs2_recv, 12)
 
     arrived(f_recv, 9)
-    fields = f_recv[...].reshape(LAT, 128)
-    fields = jnp.concatenate([fields, jnp.zeros((LATP - LAT, 128), F32)], axis=0).T
+    pairs_v[...] = f_recv[...].reshape(2 * MP, 128)
+    for half in range(2):
+        block = pairs_v[pl.ds(half, MP, stride=2), :]
+        rows_v[pl.ds(2 * half, MP, stride=TILE), :] = block
+        rows_v[pl.ds(2 * half + 1, MP, stride=TILE), :] = pltpu.roll(block, 64, 1)
+    fields = jnp.concatenate([rows_v[...], jnp.zeros((LATP - LAT, 128), F32)], axis=0).T
     fld_v[...] = fields[0:FIELDS, :]
-    to_near(fld_v, fld_near, ((0, -1), (1, 1)), 2)
-    to_near(fld_v.at[pl.ds(64, 16)], fld_far, ((0, -2), (1, 2)), 3)
-    own_part = part_v[pl.ds(pl.multiple_of(e * 16, 16), 16), :]
+    for t in range(SLOTS):
+        n, at = t + 1, t * (t + 1) // 2
+        for base, field in ((0, 8 * t), (10, 32 + 8 * t)):
+            fldn_s[0, base + at : base + at + n, :] = fld_v[field + KB - n : field + KB, :]
+            fldn_s[1, base + at : base + at + n, :] = fld_v[field : field + n, :]
+    to_near(fldn_s.at[0], fld_near, ((0, -1),), 2)
+    to_near(fldn_s.at[1], fld_near, ((1, 1),), 2)
     arrived(rs_recv, 4)
-    total = own_part
+    total = part_s[e].astype(F32)
     for d in range(ENS - 1):
-        total = total + rs_recv[d]
+        total = total + rs_recv[d].astype(F32)
     inc_v[:, 0:128] = total[0:8]
     inc_v[:, 128:256] = total[8:16]
     to_near(inc_v, halo_recv, ((0, -2), (1, -1), (2, 1), (3, 2)), 5)
+    arrived(rs2_recv, 12)
+    total = part2_s[e].astype(F32)
+    for d in range(ENS - 1):
+        total = total + rs2_recv[d].astype(F32)
+    inc2_v[...] = total
+    to_near(inc2_v, halo2_recv, ((0, -1), (1, 1)), 13)
     arrived(fld_near, 2)
-    arrived(fld_far, 3)
+    arrived(fldw_recv, 3)
+    near = [fldw_recv[n].astype(F32) for n in range(4)]
     inside = (iota((KROWS, LATP), 1) < LAT) & (iota((KROWS, LATP), 0) < 22)
     blank = jnp.zeros((2, LATP), F32)
     winds = []
@@ -269,9 +352,8 @@
         winds.append(
             jnp.concatenate(
                 [
-                    fld_far[0, at + 4 : at + 6, :], fld_near[0, 64 + at : 70 + at, :],
-                    fld_v[64 + at : 70 + at, :], fld_near[1, 64 + at : 70 + at, :],
-                    fld_far[1, at : at + 2, :], blank,
+                    near[0][at + 4 : at + 6], near[1][at : at + 6], fldw_v[at : at + 6, :],
+                    near[2][at : at + 6], near[3][at : at + 2], blank,
                 ],
                 axis=0,
             )
@@ -285,10 +367,11 @@
     for n, coef in enumerate(coefs):
         coef_v[n] = jnp.where(inside, coef, 0.0)
     for t in range(SLOTS):
-        for full, base in ((dfull_v, 8 * t), (bfull_v, 32 + 8 * t)):
-            full[t, 2:8, :] = fld_near[0, base : base + 6, :]
-            full[t, 8:14, :] = fld_v[base : base + 6, :]
-            full[t, 14:20, :] = fld_near[1, base : base + 6, :]
+        n, at = t + 1, t * (t + 1) // 2
+        for full, base, field in ((dfull_v, at, 8 * t), (bfull_v, 10 + at, 32 + 8 * t)):
+            full[t, 8 - n : 8, :] = fld_near[0, base : base + n, :]
+            full[t, 8:14, :] = fld_v[field : field + KB, :]
+            full[t, 14 : 14 + n, :] = fld_near[1, base : base + n, :]
 
     arrived(halo_recv, 5)
     state_v[0, 0:2, :] = halo_recv[0, 4:6, :]
@@ -317,11 +400,6 @@
             + from_south * below(quantity) + from_north * above(quantity)
         )
         state_v[t] = quantity
-        for n, piece in enumerate(split3(quantity[8:14, :])):
-            parts_v[32 * n + 8 * t : 32 * n + 8 * t + 6, :] = piece
-
-    s_send[...] = parts_v[...].T[0:LAT, :].reshape(PLANES, PLANE, TILE, 128).astype(BF16)
-    to_all(s_send, s_recv, 6)
 
     sens = jnp.zeros((KROWS, LATP), F32)
     for t in reversed(range(SLOTS)):
@@ -330,32 +408,83 @@
             center * sens + east_of(from_west * sens) + west(from_east * sens)
             + above(from_south * sens) + below(from_north * sens)
         )
-    ag_send[0:KB, :] = sens[8:14, :]
-
-    def send_level(d, carry):
+    own = jnp.concatenate([sens[8:14, :], jnp.zeros((2, LATP), F32)], axis=0)
+    ag_send[...] = own.astype(SENS)
+
+    for d in LEVEL_ORDER:
         pltpu.make_async_remote_copy(
             src_ref=ag_send, dst_ref=ag_recv.at[e],
             send_sem=send_sem.at[7], recv_sem=recv_sem.at[7],
             device_id={"ens": (e + d) % ENS}, device_id_type=MESH,
         ).start()
-        return carry
-
-    lax.fori_loop(1, ENS, send_level, 0)
     pltpu.make_async_copy(ag_send, ag_recv.at[e], recv_sem.at[7]).start()
+
+    arrived(wind_recv, 11)
+    row = iota((TROWS, WIDE), 0)
+    globe = row + (TILE * q - TILE)
+    inside = (globe >= 0) & (globe < LAT) & (row < 12)
+    slabs = [wind_recv[0], wind_v[...], wind_recv[1]]
+    blank = jnp.zeros((TILE, WIDE), F32)
+    east = jnp.concatenate([slab[0:4] for slab in slabs] + [blank], axis=0)
+    north = jnp.concatenate([slab[4:8] for slab in slabs] + [blank], axis=0)
+    coefs = (
+        1.0 - jnp.abs(east) - jnp.abs(north),
+        jnp.maximum(east, 0.0), jnp.maximum(-east, 0.0),
+        jnp.maximum(north, 0.0), jnp.maximum(-north, 0.0),
+    )
+    for n, coef in enumerate(coefs):
+        coef2_v[n] = jnp.where(inside, coef, 0.0)
+    arrived(halo2_recv, 13)
+    for s in range(3):
+        for c in range(3):
+            if s == 1:
+                piece = inc2_v[4 * c : 4 * c + 4, :]
+            else:
+                piece = halo2_recv[s // 2, 4 * c : 4 * c + 4, :]
+            state2_v[4 * s : 4 * s + 4, 128 * c : 128 * (c + 1)] = piece
+    lane = iota((TROWS, WIDE), 1) & 7
+    first, last = lane == 0, lane == KB - 1
+    center, from_west, from_east, from_south, from_north = [coef2_v[n] for n in range(5)]
+    quantity = jnp.where(inside, state2_v[...], 0.0)
+    sampled = []
+    for t in range(SLOTS):
+        quantity = (
+            center * quantity
+            + from_west
+            * jnp.where(first, pltpu.roll(quantity, 3, 1), pltpu.roll(quantity, 1, 1))
+            + from_east
+            * jnp.where(
+                last, pltpu.roll(quantity, WIDE - 3, 1), pltpu.roll(quantity, WIDE - 1, 1)
+            )
+            + from_south * pltpu.roll(quantity, 1, 0)
+            + from_north * pltpu.roll(quantity, TROWS - 1, 0)
+        )
+        sampled.append(quantity[4:8, :])
+    for h in range(2):
+        pair = jnp.concatenate(sampled[2 * h : 2 * h + 2], axis=0)
+        place = jnp.concatenate(places[2 * h : 2 * h + 2], axis=0)
+        value = jnp.zeros((8, OBS), F32)
+        for c in range(3):
+            picked = jnp.take_along_axis(pair[:, 128 * c : 128 * (c + 1)], place & 127, axis=1)
+            value = jnp.where((place >> 7) == c, picked, value)
+        dep_v[8 * h : 8 * h + 8, :] = value - jnp.concatenate(observed[2 * h : 2 * h + 2], axis=0)
 
     sent(a1_mid.at[pl.ds(0, PLANE - 1)], 0)
     sent(a1_recv.at[pl.ds(0, PLANES - 1)], 8)
-    sent(f_mid.at[pl.ds(0, PLANE - 1)], 1)
-    sent(f_recv.at[pl.ds(0, PLANES - 1)], 9)
-    sent(fld_near, 2)
-    sent(fld_far, 3)
-    sent(rs_recv, 4)
-    sent(halo_recv, 5)
+    for middle, last_ref, n, m in ((b_mid, b_recv, 6, 10), (f_mid, f_recv, 1, 9)):
+        sent(middle.at[pl.ds(0, PLANES - 1)], n)
+        sent(last_ref.at[:, pl.ds(0, PLANE - 1)], m)
+    for ref, n in (
+        (fld_near, 2), (fldw_recv, 3), (rs_recv, 4), (halo_recv, 5), (wind_recv, 11),
+        (rs2_recv, 12), (halo2_recv, 13),
+    ):
+        sent(ref, n)
 
     arrived(ag_recv, 7)
+    level_v[...] = ag_recv[...].astype(F32)
     products = jnp.concatenate(
         [
-            (ensk_v[LEV * k : LEV * (k + 1), :] * ag_recv[:, k, :]).astype(BF16).astype(F32)
+            (ensk_v[LEV * k : LEV * (k + 1), :] * level_v[:, k, :]).astype(BF16).astype(F32)
             for k in range(KB)
         ],
         axis=0,
@@ -363,33 +492,6 @@
     smooth = jnp.dot(products, kern_v[...], preferred_element_type=F32)
     grad_v[...] = smooth[:, 0:LAT] + ctl_v[...].astype(F32)
 
-    arrived(s_recv, 6)
-    states = s_recv[...].astype(F32).reshape(LAT, 128)
-    states = jnp.concatenate([states, jnp.zeros((LATP - LAT, 128), F32)], axis=0).T
-    samp_v[...] = states[0:32, :] + states[32:64, :] + states[64:96, :]
-    tile_row = iota((8, OBS), 0) & 3
-    for h in range(2):
-        block = jnp.concatenate(blocks[2 * h : 2 * h + 2], axis=0)
-        lon_in = jnp.concatenate(inner[2 * h : 2 * h + 2], axis=0)
-        index = TILE * block + tile_row
-        within, half = index & 127, index >> 7
-        sampled = jnp.zeros((8, OBS), F32)
-        for k in range(KB):
-            at = 16 * h + k
-            both = jnp.concatenate(
-                [
-                    jnp.broadcast_to(samp_v[at : at + 1, :], (TILE, LATP)),
-                    jnp.broadcast_to(samp_v[at + 8 : at + 9, :], (TILE, LATP)),
-                ],
-                axis=0,
-            )
-            low = jnp.take_along_axis(both[:, 0:128], within, axis=1)
-            high = jnp.take_along_axis(both[:, 128:256], within, axis=1)
-            sampled = jnp.where(lon_in == k, jnp.where(half == 0, low, high), sampled)
-        dep_v[8 * h : 8 * h + 8, :] = sampled - jnp.concatenate(observed[2 * h : 2 * h + 2], axis=0)
-    sent(s_recv.at[0], 6)
-    sent(s_recv.at[1], 6)
-    sent(s_recv.at[2, pl.ds(0, PLANE - 1)], 6)
     sent(ag_recv.at[pl.ds(0, ENS - 1)], 7)
 
 
@@ -435,30 +537,45 @@
         pltpu.VMEM((PLANES, PLANE, TILE, 128), BF16),
         pltpu.VMEM((PLANE, PLANES, TILE, 128), BF16),
         pltpu.VMEM((PLANES, PLANE, TILE, 128), BF16),
-        pltpu.VMEM((TILE, 128, WIDE), F32),
-        pltpu.VMEM((PLANES, PLANE, TILE, 128), F32),
-        pltpu.VMEM((PLANE, PLANES, TILE, 128), F32),
-        pltpu.VMEM((PLANES, PLANE, TILE, 128), F32),
+        pltpu.VMEM((3, 128, WIDE), F32),
+        pltpu.VMEM((PLANES, PLANE, 2, 128), F32),
+        pltpu.VMEM((PLANES, PLANE, 2, 128), F32),
+        pltpu.VMEM((PLANES, PLANE, 2, 128), F32),
         pltpu.VMEM((FIELDS, LATP), F32),
-        pltpu.VMEM((2, FIELDS, LATP), F32),
-        pltpu.VMEM((2, 16, LATP), F32),
+        pltpu.VMEM((2, 24, LATP), F32),
+        pltpu.VMEM((2, 24, LATP), F32),
+        pltpu.VMEM((16, LATP), F32),
+        pltpu.VMEM((16, LATP), BF16),
+        pltpu.VMEM((4, 16, LATP), BF16),
+        pltpu.VMEM((2 * MP, 128), F32),
         pltpu.VMEM((LEV * 16, 128), F32),
-        pltpu.VMEM((ENS - 1, 16, 128), F32),
+        pltpu.VMEM((LEV, 16, 128), PART),
+        pltpu.VMEM((ENS - 1, 16, 128), PART),
         pltpu.VMEM((8, LATP), F32),
         pltpu.VMEM((4, 8, LATP), F32),
         pltpu.VMEM((SLOTS, KROWS, LATP), F32),
         pltpu.VMEM((5, KROWS, LATP), F32),
         pltpu.VMEM((SLOTS, KROWS, LATP), F32),
         pltpu.VMEM((SLOTS, KROWS, LATP), F32),
-        pltpu.VMEM((128, LATP), F32),
+        pltpu.VMEM((8, LATP), SENS),
+        pltpu.VMEM((ENS, 8, LATP), SENS),
+        pltpu.VMEM((ENS, 8, LATP), F32),
+        pltpu.VMEM((TILE * LEV, WIDE), F32),
         pltpu.VMEM((PLANES, PLANE, TILE, 128), BF16),
         pltpu.VMEM((PLANES, PLANE, TILE, 128), BF16),
-        pltpu.VMEM((8, LATP), F32),
-        pltpu.VMEM((ENS, 8, LATP), F32),
-        pltpu.VMEM((32, LATP), F32),
+        pltpu.VMEM((PLANES, PLANE, TILE, 128), BF16),
+        pltpu.VMEM((LEV * 16, 128), F32),
+        pltpu.VMEM((LEV, 16, 128), PART2),
+        pltpu.VMEM((ENS - 1, 16, 128), PART2),
+        pltpu.VMEM((16, 128), F32),
+        pltpu.VMEM((2, 16, 128), F32),
+        pltpu.VMEM((8, WIDE), F32),
+        pltpu.VMEM((2, 8, WIDE), F32),
+        pltpu.VMEM((TROWS, WIDE), F32),
+        pltpu.VMEM((5, TROWS, WIDE), F32),
         pltpu.SemaphoreType.DMA((8,)),
-        pltpu.SemaphoreType.DMA((10,)),
-        pltpu.SemaphoreType.DMA((10,)),
+        pltpu.SemaphoreType.DMA((14,)),
+        pltpu.SemaphoreType.DMA((14,)),
     ]
     gradient, departures = pl.pallas_call(
         body,

time: 52 us -> 46.1 us (0.89)
  Pallas kernels: 51.2 us -> 45.1 us
    pallas_call x1, Pallas kernels: 50.5 us -> 44.4 us  [shards(): pl.pallas_call(body, out_shape=outs, in_specs=[anywhere] * len(operands),...]
where the time goes in v4:
time: 46.1 us; the launch traced here: 45.7 us
  Pallas kernels  45.1 us (98%)
  between operations  0.64 us (1%)
    pallas_call x1, Pallas kernels, shards(): pl.pallas_call(body, out_shape=outs, in_specs=[anywhere] * len(operands),...  44.4 us

profile of v4, /device:TPU:1, one launch (start us, length us, event | category | flops | bytes accessed | tf_op | source)
XLA Modules:
  0.0 45.7 jit_solution(3994866794877238436)
XLA Ops:
  0.6 44.4 %assimilate.1 = (f32[96,192]{1,0:T(8,128)S(1)}, f32[16,128]{1,0:T(8,128)S(1)}) custom-call(bf16[64,288]{1,0:T(8,128)(2,1)} %bitcast.15, bf16[96,192]{1,0:T(8,128)(2,1)} %bitcast.16, s32[1,192]{1,0:T(1,128)} %bitcast.19, bf16[64,288]{1,0:T(8,128)(2,1)} %bitcast.17, bf16[64,288]{1,0:T(8,128)(2,1)} %bitcast.18, s32[4,4,128]{2,1,0:T(4,128)} %lon_hbm.1, ...), custom_call_target="tpu_custom_call" | custom-call | tf_op jit(solution)/shard_map/assimilate/pallas_call | solution.py:580
  45.0 0.7 %move_out.1 = (f32[96,192]{1,0:T(8,128)}, f32[16,128]{1,0:T(8,128)}) custom-call(f32[96,192]{1,0:T(8,128)S(1)} %get-tuple-element.6.grad_v, f32[16,128]{1,0:T(8,128)S(1)} %get-tuple-element.7.dep_v), custom_call_target="tpu_custom_call" | custom-call | tf_op jit(solution)/shard_map/move_out/pallas_call | solution.py:591

commit v5 on v4

--- a/solution.py
+++ b/solution.py
@@ -39,11 +39,11 @@
     grad_v, dep_v,
     ens_v, ctl_v, band_v, east_v, north_v, lon_v, inn_v, wgt_v,
     kern_v, rows_v, wide_v, spread_v, ensk_v, embed_v,
-    a1_send, a1_mid, a1_recv, sparse_v, f_send, f_mid, f_recv, fld_v, fldn_s, fld_near, fldw_v, fldw_s, fldw_recv, pairs_v,
-    part_v, part_s, rs_recv, inc_v, halo_recv, state_v, coef_v, dfull_v, bfull_v,
+    a1_send, a1_mid, a1_recv, sparse_v, f_send, f_mid, f_recv, fld_v, edge_v, fldn_s, fld_near, fldw_v, fldw_s, fldw_recv, pairs_v,
+    part_v, part_s, rs_recv, inc_v, halo_recv, inc_far_s, halo_far, state_v, coef_v, dfull_v, bfull_v,
     ag_send, ag_recv, level_v,
     ensw_v, b_send, b_mid, b_recv, part2_v, part2_s, rs2_recv, inc2_v, halo2_recv,
-    wind_v, wind_recv, state2_v, coef2_v,
+    wind_v, wind_s, wind_recv, state2_v, coef2_v,
     in_sem, send_sem, recv_sem,
 ):
     q = lax.axis_index("mp")
@@ -52,28 +52,15 @@
 
     barrier = pltpu.get_barrier_semaphore()
 
-    def greet_plane(d, carry):
-        pl.semaphore_signal(
-            barrier, inc=1, device_id={"mp": plane * PLANE + (rank + d) % PLANE},
-            device_id_type=MESH,
-        )
-        return carry
-
-    def greet_line(d, carry):
-        pl.semaphore_signal(
-            barrier, inc=1, device_id={"mp": (q + PLANE * d) % MP}, device_id_type=MESH
-        )
-        return carry
-
-    def greet_ens(d, carry):
-        pl.semaphore_signal(
-            barrier, inc=1, device_id={"ens": (e + d) % ENS}, device_id_type=MESH
-        )
-        return carry
-
-    lax.fori_loop(1, ENS, greet_ens, 0)
-    lax.fori_loop(1, PLANES, greet_line, 0)
-    lax.fori_loop(1, PLANE, greet_plane, 0)
+    def greet(device):
+        pl.semaphore_signal(barrier, inc=1, device_id=device, device_id_type=MESH)
+
+    for d in LEVEL_ORDER:
+        greet({"ens": (e + d) % ENS})
+    for d in range(1, PLANES):
+        greet({"mp": (q + PLANE * d) % MP})
+    for d in LEVEL_ORDER:
+        greet({"mp": plane * PLANE + (rank + d) % PLANE})
     pairs = [
         (ens_hbm, ens_v), (ctl_hbm, ctl_v), (band_hbm, band_v), (east_hbm, east_v),
         (north_hbm, north_v), (lon_hbm, lon_v), (inn_hbm, inn_v), (wgt_hbm, wgt_v),
@@ -99,103 +86,6 @@
     ensw_v[...] = padded
     wide_v[...] = jnp.concatenate([padded, jnp.zeros((128 - TILE * LEV, WIDE), F32)], axis=0).T
     by_lon = [wide_v[pl.ds(k, MP, stride=8), :] for k in range(KB)]
-    for i in range(TILE):
-        block = jnp.zeros((MP, 128), F32)
-        for k in range(KB):
-            block = jnp.where(group == k, pltpu.roll(by_lon[k], (16 * (k - i)) % 128, 1), block)
-        rows_v[pl.ds(i, MP, stride=TILE), :] = block
-    a1_send[...] = rows_v[...].reshape(PLANES, PLANE, TILE, 128).astype(BF16)
-
-    pl.semaphore_wait(barrier, PLANE + PLANES + ENS - 3)
-
-    def to_plane(src, middle, n):
-        def send(d, carry):
-            to = (rank + d) % PLANE
-            pltpu.make_async_remote_copy(
-                src_ref=src.at[:, to], dst_ref=middle.at[rank],
-                send_sem=send_sem.at[n], recv_sem=recv_sem.at[n],
-                device_id={"mp": plane * PLANE + to}, device_id_type=MESH,
-            ).start()
-            return carry
-
-        lax.fori_loop(1, PLANE, send, 0)
-        pltpu.make_async_copy(src.at[:, rank], middle.at[rank], recv_sem.at[n]).start()
-
-    def to_line(middle, dst, n):
-        for d in range(1, PLANES):
-            to = (plane + d) % PLANES
-            pltpu.make_async_remote_copy(
-                src_ref=middle.at[:, to], dst_ref=dst.at[plane],
-                send_sem=send_sem.at[n], recv_sem=recv_sem.at[n],
-                device_id={"mp": to * PLANE + rank}, device_id_type=MESH,
-            ).start()
-        pltpu.make_async_copy(middle.at[:, plane], dst.at[plane], recv_sem.at[n]).start()
-
-    def line_first(src, middle, n):
-        for d in range(1, PLANES):
-            to = (plane + d) % PLANES
-            pltpu.make_async_remote_copy(
-                src_ref=src.at[to], dst_ref=middle.at[plane],
-                send_sem=send_sem.at[n], recv_sem=recv_sem.at[n],
-                device_id={"mp": to * PLANE + rank}, device_id_type=MESH,
-            ).start()
-        pltpu.make_async_copy(src.at[plane], middle.at[plane], recv_sem.at[n]).start()
-
-    def plane_next(middle, dst, n):
-        def send(d, carry):
-            to = (rank + d) % PLANE
-            pltpu.make_async_remote_copy(
-                src_ref=middle.at[:, to], dst_ref=dst.at[:, rank],
-                send_sem=send_sem.at[n], recv_sem=recv_sem.at[n],
-                device_id={"mp": plane * PLANE + to}, device_id_type=MESH,
-            ).start()
-            return carry
-
-        lax.fori_loop(1, PLANE, send, 0)
-        pltpu.make_async_copy(middle.at[:, rank], dst.at[:, rank], recv_sem.at[n]).start()
-
-    def to_near(src, dst, slots, n):
-        for slot, offset in slots:
-            pltpu.make_async_remote_copy(
-                src_ref=src, dst_ref=dst.at[slot], send_sem=send_sem.at[n],
-                recv_sem=recv_sem.at[n],
-                device_id={"mp": (q - offset + MP) % MP}, device_id_type=MESH,
-            ).start()
-
-    def arrived(ref, n):
-        pltpu.make_async_copy(ref, ref, recv_sem.at[n]).wait()
-
-    def sent(ref, n):
-        pltpu.make_async_copy(ref, ref, send_sem.at[n]).wait()
-
-    to_plane(a1_send, a1_mid, 0)
-
-    for copy in loads[1:3]:
-        copy.wait()
-    band = jnp.concatenate([band_v[...].astype(F32), jnp.ones((1, LATP - LAT), F32)], axis=1)
-    width_j = jnp.broadcast_to(band, (LATP, LATP))
-    width_i = width_j.T
-    row, column = iota((LATP, LATP), 0), iota((LATP, LATP), 1)
-    distance = jnp.abs(row - column).astype(F32)
-    weights = jnp.maximum(0.0, 1.0 - 2.0 * distance / (width_i + width_j))
-    kern_v[...] = jnp.where((row < LAT) & (column < LAT), weights, 0.0).astype(BF16)
-    spread = jnp.dot(ctl_v[...], kern_v[0:LAT, :], preferred_element_type=F32)
-    spread_v[...] = spread.astype(BF16).astype(F32)
-
-
-    by_tile = lax.dot_general(
-        kern_v[0:LAT, 0:LAT], ctl_v[...], (((1,), (1,)), ((), ())), preferred_element_type=F32
-    )
-    rows_v[...] = jnp.concatenate([by_tile, jnp.zeros((LAT, 128 - KB * LEV), F32)], axis=1)
-    by_row = [rows_v[pl.ds(i, MP, stride=TILE), :] for i in range(TILE)]
-    for r in range(TILE - 1):
-        block = jnp.zeros((MP, 128), F32)
-        for h in range(2):
-            k = 2 * r + h
-            for i in range(TILE):
-                moved = pltpu.roll(by_row[i], (64 * h + 16 * (i - k)) % 128, 1)
-                block = jnp.where(group == 4 * h + i, moved, block)
-        rows_v[pl.ds(r, MP, stride=TILE), :] = block
     for copy in loads[3:5]:
         copy.wait()
     mine = iota((LEV, LON), 0) == e
@@ -208,6 +98,7 @@
         jnp.concatenate(winds, axis=0).astype(BF16), embed_v[...], preferred_element_type=F32
     )
     wind_v[...] = wide_winds
+    wind_s[...] = wide_winds.astype(BF16)
     for i in range(TILE):
         sparse_v[0, 16 * i : 16 * i + 1, :] = wide_winds[i : i + 1]
         sparse_v[0, 16 * i + 8 : 16 * i + 9, :] = wide_winds[TILE + i : TILE + i + 1]
@@ -219,9 +110,13 @@
             total = total + pltpu.roll(wide_v[pl.ds(k, MP, stride=8), :], k, 1)
         return total
 
-    rows_v[pl.ds(3, MP, stride=TILE), :] = spaced(0)
-    b_send[...] = rows_v[...].reshape(PLANES, PLANE, TILE, 128).astype(BF16)
-    line_first(b_send, b_mid, 6)
+    wind_lanes = spaced(0)
+    for i in range(TILE):
+        block = jnp.where(group == 6, pltpu.roll(wind_lanes, (96 - 16 * i) % 128, 1), 0.0)
+        for k in range(KB):
+            block = jnp.where(group == k, pltpu.roll(by_lon[k], (16 * (k - i)) % 128, 1), block)
+        rows_v[pl.ds(i, MP, stride=TILE), :] = block
+    a1_send[...] = rows_v[...].reshape(PLANES, PLANE, TILE, 128).astype(BF16)
 
     for copy in loads[5:]:
         copy.wait()
@@ -260,14 +155,104 @@
     for half in range(2):
         pairs_v[pl.ds(half, MP, stride=2), :] = spaced(1 + half)
     f_send[...] = pairs_v[...].reshape(PLANES, PLANE, 2, 128)
+    pl.semaphore_wait(barrier, PLANE + PLANES + ENS - 3)
+
+    def to_plane(src, middle, n):
+        for d in LEVEL_ORDER:
+            to = (rank + d) % PLANE
+            pltpu.make_async_remote_copy(
+                src_ref=src.at[:, to], dst_ref=middle.at[rank],
+                send_sem=send_sem.at[n], recv_sem=recv_sem.at[n],
+                device_id={"mp": plane * PLANE + to}, device_id_type=MESH,
+            ).start()
+        pltpu.make_async_copy(src.at[:, rank], middle.at[rank], recv_sem.at[n]).start()
+
+    def to_line(middle, dst, n):
+        for d in range(1, PLANES):
+            to = (plane + d) % PLANES
+            pltpu.make_async_remote_copy(
+                src_ref=middle.at[:, to], dst_ref=dst.at[plane],
+                send_sem=send_sem.at[n], recv_sem=recv_sem.at[n],
+                device_id={"mp": to * PLANE + rank}, device_id_type=MESH,
+            ).start()
+        pltpu.make_async_copy(middle.at[:, plane], dst.at[plane], recv_sem.at[n]).start()
+
+    def line_first(src, middle, n):
+        for d in range(1, PLANES):
+            to = (plane + d) % PLANES
+            pltpu.make_async_remote_copy(
+                src_ref=src.at[to], dst_ref=middle.at[plane],
+                send_sem=send_sem.at[n], recv_sem=recv_sem.at[n],
+                device_id={"mp": to * PLANE + rank}, device_id_type=MESH,
+            ).start()
+        pltpu.make_async_copy(src.at[plane], middle.at[plane], recv_sem.at[n]).start()
+
+    def plane_next(middle, dst, n):
+        def send(d, carry):
+            to = (rank + d) % PLANE
+            pltpu.make_async_remote_copy(
+                src_ref=middle.at[:, to], dst_ref=dst.at[:, rank],
+                send_sem=send_sem.at[n], recv_sem=recv_sem.at[n],
+                device_id={"mp": plane * PLANE + to}, device_id_type=MESH,
+            ).start()
+            return carry
+
+        lax.fori_loop(1, PLANE, send, 0)
+        pltpu.make_async_copy(middle.at[:, rank], dst.at[:, rank], recv_sem.at[n]).start()
+
+    def to_near(src, dst, slots, n):
+        for slot, offset in slots:
+            pltpu.make_async_remote_copy(
+                src_ref=src, dst_ref=dst.at[slot], send_sem=send_sem.at[n],
+                recv_sem=recv_sem.at[n],
+                device_id={"mp": (q - offset + MP) % MP}, device_id_type=MESH,
+            ).start()
+
+    def arrived(ref, n):
+        pltpu.make_async_copy(ref, ref, recv_sem.at[n]).wait()
+
+    def sent(ref, n):
+        pltpu.make_async_copy(ref, ref, send_sem.at[n]).wait()
+
+    to_plane(a1_send, a1_mid, 0)
     line_first(f_send, f_mid, 1)
+
+    for copy in loads[1:3]:
+        copy.wait()
+    band = jnp.concatenate([band_v[...].astype(F32), jnp.ones((1, LATP - LAT), F32)], axis=1)
+    width_j = jnp.broadcast_to(band, (LATP, LATP))
+    width_i = width_j.T
+    row, column = iota((LATP, LATP), 0), iota((LATP, LATP), 1)
+    distance = jnp.abs(row - column).astype(F32)
+    weights = jnp.maximum(0.0, 1.0 - 2.0 * distance / (width_i + width_j))
+    kern_v[...] = jnp.where((row < LAT) & (column < LAT), weights, 0.0).astype(BF16)
+    spread = jnp.dot(ctl_v[...], kern_v[0:LAT, :], preferred_element_type=F32)
+    spread_v[...] = spread.astype(BF16).astype(F32)
+
+
+    by_tile = lax.dot_general(
+        kern_v[0:LAT, 0:LAT], ctl_v[...], (((1,), (1,)), ((), ())), preferred_element_type=F32
+    )
+    rows_v[...] = jnp.concatenate([by_tile, jnp.zeros((LAT, 128 - KB * LEV), F32)], axis=1)
+    by_row = [rows_v[pl.ds(i, MP, stride=TILE), :] for i in range(TILE)]
+    for r in range(TILE - 1):
+        block = jnp.zeros((MP, 128), F32)
+        for h in range(2):
+            k = 2 * r + h
+            for i in range(TILE):
+                moved = pltpu.roll(by_row[i], (64 * h + 16 * (i - k)) % 128, 1)
+                block = jnp.where(group == 4 * h + i, moved, block)
+        rows_v[pl.ds(r, MP, stride=TILE), :] = block
+    b_send[...] = rows_v[...].reshape(PLANES, PLANE, TILE, 128).astype(BF16)
+    line_first(b_send, b_mid, 6)
+
+
     arrived(a1_mid, 0)
     to_line(a1_mid, a1_recv, 8)
-
+    arrived(f_mid, 1)
+    plane_next(f_mid, f_recv, 9)
     arrived(b_mid, 6)
     plane_next(b_mid, b_recv, 10)
-    arrived(f_mid, 1)
-    plane_next(f_mid, f_recv, 9)
     arrived(a1_recv, 8)
     gathered = a1_recv[...].astype(F32).reshape(LAT, 128)
     ensk = jnp.concatenate([gathered, jnp.zeros((LATP - LAT, 128), F32)], axis=0).T
@@ -291,28 +276,10 @@
             ).start()
 
     to_levels(part_s, rs_recv, 4)
-    to_near(wind_v, wind_recv, ((0, -1), (1, 1)), 11)
-
-    arrived(b_recv, 10)
-    rows_v[...] = b_recv[...].astype(F32).reshape(LAT, 128)
-    for r in range(KB // 2):
-        block = rows_v[pl.ds(r, MP, stride=TILE), :]
-        wide_v[pl.ds(2 * r, MP, stride=8), :] = block
-        wide_v[pl.ds(2 * r + 1, MP, stride=8), :] = pltpu.roll(block, 64, 1)
-    native = wide_v[...].T
-    by_block = rows_v[pl.ds(3, MP, stride=TILE), :]
-    for i in range(TILE):
-        rows_v[pl.ds(i, MP, stride=TILE), :] = pltpu.roll(by_block, (-16 * i) % 128, 1)
-    fields = jnp.concatenate([rows_v[...], jnp.zeros((LATP - LAT, 128), F32)], axis=0).T
-    fldw_v[...] = fields[0:16, :]
-    fldw_s[...] = fields[0:16, :].astype(BF16)
+    fldw_v[...] = ensk[96:112, :]
+    fldw_s[...] = ensk[96:112, :].astype(BF16)
     to_near(fldw_s, fldw_recv, ((0, -2), (1, -1), (2, 1), (3, 2)), 3)
-    for i in range(TILE):
-        own = ensw_v[LEV * i : LEV * (i + 1), :] * native[LEV * i : LEV * (i + 1), :]
-        for c in range(3):
-            part2_v[pl.ds(4 * c + i, LEV, stride=16), :] = own[:, 128 * c : 128 * (c + 1)]
-    part2_s[...] = part2_v[...].reshape(LEV, 16, 128).astype(PART2)
-    to_levels(part2_s, rs2_recv, 12)
+    to_near(wind_s, wind_recv, ((0, -1), (1, 1)), 11)
 
     arrived(f_recv, 9)
     pairs_v[...] = f_recv[...].reshape(2 * MP, 128)
@@ -325,17 +292,40 @@
     for t in range(SLOTS):
         n, at = t + 1, t * (t + 1) // 2
         for base, field in ((0, 8 * t), (10, 32 + 8 * t)):
-            fldn_s[0, base + at : base + at + n, :] = fld_v[field + KB - n : field + KB, :]
-            fldn_s[1, base + at : base + at + n, :] = fld_v[field : field + n, :]
+            edge_v[0, base + at : base + at + n, :] = fld_v[field + KB - n : field + KB, :]
+            edge_v[1, base + at : base + at + n, :] = fld_v[field : field + n, :]
+    for side in range(2):
+        fldn_s[side, 0:20, :] = edge_v[side, 0:20, 0:128]
+        fldn_s[side, 20:30, :] = edge_v[side, 0:10, 128:256] + pltpu.roll(
+            edge_v[side, 10:20, 128:256], 64, 1
+        )
     to_near(fldn_s.at[0], fld_near, ((0, -1),), 2)
     to_near(fldn_s.at[1], fld_near, ((1, 1),), 2)
+    arrived(b_recv, 10)
+    rows_v[...] = b_recv[...].astype(F32).reshape(LAT, 128)
+    for r in range(KB // 2):
+        block = rows_v[pl.ds(r, MP, stride=TILE), :]
+        wide_v[pl.ds(2 * r, MP, stride=8), :] = block
+        wide_v[pl.ds(2 * r + 1, MP, stride=8), :] = pltpu.roll(block, 64, 1)
+    native = wide_v[...].T
+    for i in range(TILE):
+        own = ensw_v[LEV * i : LEV * (i + 1), :] * native[LEV * i : LEV * (i + 1), :]
+        for c in range(3):
+            part2_v[pl.ds(4 * c + i, LEV, stride=16), :] = own[:, 128 * c : 128 * (c + 1)]
+    part2_s[...] = part2_v[...].reshape(LEV, 16, 128).astype(PART2)
+    to_levels(part2_s, rs2_recv, 12)
+
     arrived(rs_recv, 4)
     total = part_s[e].astype(F32)
     for d in range(ENS - 1):
         total = total + rs_recv[d].astype(F32)
     inc_v[:, 0:128] = total[0:8]
     inc_v[:, 128:256] = total[8:16]
-    to_near(inc_v, halo_recv, ((0, -2), (1, -1), (2, 1), (3, 2)), 5)
+    inc_far_s[0] = inc_v[4:6, :]
+    inc_far_s[1] = inc_v[0:2, :]
+    to_near(inc_v, halo_recv, ((0, -1), (1, 1)), 5)
+    to_near(inc_far_s.at[0], halo_far, ((0, -2),), 14)
+    to_near(inc_far_s.at[1], halo_far, ((1, 2),), 14)
     arrived(rs2_recv, 12)
     total = part2_s[e].astype(F32)
     for d in range(ENS - 1):
@@ -345,6 +335,12 @@
     arrived(fld_near, 2)
     arrived(fldw_recv, 3)
     near = [fldw_recv[n].astype(F32) for n in range(4)]
+    low_half = iota((10, 128), 1) < 64
+    for side in range(2):
+        rest = fld_near[side, 20:30, :]
+        edge_v[side, 0:20, 0:128] = fld_near[side, 0:20, :]
+        edge_v[side, 0:10, 128:256] = jnp.where(low_half, rest, 0.0)
+        edge_v[side, 10:20, 128:256] = jnp.where(low_half, pltpu.roll(rest, 64, 1), 0.0)
     inside = (iota((KROWS, LATP), 1) < LAT) & (iota((KROWS, LATP), 0) < 22)
     blank = jnp.zeros((2, LATP), F32)
     winds = []
@@ -369,16 +365,17 @@
     for t in range(SLOTS):
         n, at = t + 1, t * (t + 1) // 2
         for full, base, field in ((dfull_v, at, 8 * t), (bfull_v, 10 + at, 32 + 8 * t)):
-            full[t, 8 - n : 8, :] = fld_near[0, base : base + n, :]
+            full[t, 8 - n : 8, :] = edge_v[0, base : base + n, :]
             full[t, 8:14, :] = fld_v[field : field + KB, :]
-            full[t, 14 : 14 + n, :] = fld_near[1, base : base + n, :]
-
+            full[t, 14 : 14 + n, :] = edge_v[1, base : base + n, :]
+
+    state_v[0, 8:14, :] = inc_v[0:6, :]
     arrived(halo_recv, 5)
-    state_v[0, 0:2, :] = halo_recv[0, 4:6, :]
-    state_v[0, 2:8, :] = halo_recv[1, 0:6, :]
-    state_v[0, 8:14, :] = inc_v[0:6, :]
-    state_v[0, 14:20, :] = halo_recv[2, 0:6, :]
-    state_v[0, 20:22, :] = halo_recv[3, 0:2, :]
+    arrived(halo_far, 14)
+    state_v[0, 0:2, :] = halo_far[0]
+    state_v[0, 2:8, :] = halo_recv[0, 0:6, :]
+    state_v[0, 14:20, :] = halo_recv[1, 0:6, :]
+    state_v[0, 20:22, :] = halo_far[1]
 
     def west(value):
         return pltpu.roll(value, 1, 0)
@@ -423,7 +420,7 @@
     row = iota((TROWS, WIDE), 0)
     globe = row + (TILE * q - TILE)
     inside = (globe >= 0) & (globe < LAT) & (row < 12)
-    slabs = [wind_recv[0], wind_v[...], wind_recv[1]]
+    slabs = [wind_recv[0].astype(F32), wind_v[...], wind_recv[1].astype(F32)]
     blank = jnp.zeros((TILE, WIDE), F32)
     east = jnp.concatenate([slab[0:4] for slab in slabs] + [blank], axis=0)
     north = jnp.concatenate([slab[4:8] for slab in slabs] + [blank], axis=0)
@@ -476,7 +473,7 @@
         sent(last_ref.at[:, pl.ds(0, PLANE - 1)], m)
     for ref, n in (
         (fld_near, 2), (fldw_recv, 3), (rs_recv, 4), (halo_recv, 5), (wind_recv, 11),
-        (rs2_recv, 12), (halo2_recv, 13),
+        (rs2_recv, 12), (halo2_recv, 13), (halo_far, 14),
     ):
         sent(ref, n)
 
@@ -543,7 +540,8 @@
         pltpu.VMEM((PLANES, PLANE, 2, 128), F32),
         pltpu.VMEM((FIELDS, LATP), F32),
         pltpu.VMEM((2, 24, LATP), F32),
-        pltpu.VMEM((2, 24, LATP), F32),
+        pltpu.VMEM((2, 32, 128), F32),
+        pltpu.VMEM((2, 32, 128), F32),
         pltpu.VMEM((16, LATP), F32),
         pltpu.VMEM((16, LATP), BF16),
         pltpu.VMEM((4, 16, LATP), BF16),
@@ -552,7 +550,9 @@
         pltpu.VMEM((LEV, 16, 128), PART),
         pltpu.VMEM((ENS - 1, 16, 128), PART),
         pltpu.VMEM((8, LATP), F32),
-        pltpu.VMEM((4, 8, LATP), F32),
+        pltpu.VMEM((2, 8, LATP), F32),
+        pltpu.VMEM((2, 2, LATP), F32),
+        pltpu.VMEM((2, 2, LATP), F32),
         pltpu.VMEM((SLOTS, KROWS, LATP), F32),
         pltpu.VMEM((5, KROWS, LATP), F32),
         pltpu.VMEM((SLOTS, KROWS, LATP), F32),
@@ -570,12 +570,13 @@
         pltpu.VMEM((16, 128), F32),
         pltpu.VMEM((2, 16, 128), F32),
         pltpu.VMEM((8, WIDE), F32),
-        pltpu.VMEM((2, 8, WIDE), F32),
+        pltpu.VMEM((8, WIDE), BF16),
+        pltpu.VMEM((2, 8, WIDE), BF16),
         pltpu.VMEM((TROWS, WIDE), F32),
         pltpu.VMEM((5, TROWS, WIDE), F32),
         pltpu.SemaphoreType.DMA((8,)),
-        pltpu.SemaphoreType.DMA((14,)),
-        pltpu.SemaphoreType.DMA((14,)),
+        pltpu.SemaphoreType.DMA((15,)),
+        pltpu.SemaphoreType.DMA((15,)),
     ]
     gradient, departures = pl.pallas_call(
         body,

time: 46.1 us -> 45.5 us (0.987)
  the two profiles are of different devices: /device:TPU:1 before, /device:TPU:56 now
where the time goes in v5:
time: 45.5 us; the launch traced here: 45.3 us
  Pallas kernels  44.7 us (98%)
  between operations  0.64 us (1%)
    pallas_call x1, Pallas kernels, shards(): pl.pallas_call(body, out_shape=outs, in_specs=[anywhere] * len(operands),...  44 us

profile of v5, /device:TPU:56, one launch (start us, length us, event | category | flops | bytes accessed | tf_op | source)
XLA Modules:
  0.0 45.3 jit_solution(3290957952787063856)
XLA Ops:
  0.6 44.0 %assimilate.1 = (f32[96,192]{1,0:T(8,128)S(1)}, f32[16,128]{1,0:T(8,128)S(1)}) custom-call(bf16[64,288]{1,0:T(8,128)(2,1)} %bitcast.15, bf16[96,192]{1,0:T(8,128)(2,1)} %bitcast.16, s32[1,192]{1,0:T(1,128)} %bitcast.19, bf16[64,288]{1,0:T(8,128)(2,1)} %bitcast.17, bf16[64,288]{1,0:T(8,128)(2,1)} %bitcast.18, s32[4,4,128]{2,1,0:T(4,128)} %lon_hbm.1, ...), custom_call_target="tpu_custom_call" | custom-call | tf_op jit(solution)/shard_map/assimilate/pallas_call | solution.py:581
  44.7 0.7 %move_out.1 = (f32[96,192]{1,0:T(8,128)}, f32[16,128]{1,0:T(8,128)}) custom-call(f32[96,192]{1,0:T(8,128)S(1)} %get-tuple-element.6.grad_v, f32[16,128]{1,0:T(8,128)S(1)} %get-tuple-element.7.dep_v), custom_call_target="tpu_custom_call" | custom-call | tf_op jit(solution)/shard_map/move_out/pallas_call | solution.py:592

commit v6 on v5

--- a/solution.py
+++ b/solution.py
@@ -66,7 +66,8 @@
         (north_hbm, north_v), (lon_hbm, lon_v), (inn_hbm, inn_v), (wgt_hbm, wgt_v),
     ]
     loads = [
-        pltpu.make_async_copy(src, dst, in_sem.at[n]) for n, (src, dst) in enumerate(pairs)
+        pltpu.make_async_copy(src, dst, in_sem.at[(0, 1, 1, 2, 2, 3, 3, 3)[n]])
+        for n, (src, dst) in enumerate(pairs)
     ]
     for copy in loads:
         copy.start()
@@ -162,7 +163,7 @@
             to = (rank + d) % PLANE
             pltpu.make_async_remote_copy(
                 src_ref=src.at[:, to], dst_ref=middle.at[rank],
-                send_sem=send_sem.at[n], recv_sem=recv_sem.at[n],
+                send_sem=send_sem.at[0], recv_sem=recv_sem.at[n],
                 device_id={"mp": plane * PLANE + to}, device_id_type=MESH,
             ).start()
         pltpu.make_async_copy(src.at[:, rank], middle.at[rank], recv_sem.at[n]).start()
@@ -172,7 +173,7 @@
             to = (plane + d) % PLANES
             pltpu.make_async_remote_copy(
                 src_ref=middle.at[:, to], dst_ref=dst.at[plane],
-                send_sem=send_sem.at[n], recv_sem=recv_sem.at[n],
+                send_sem=send_sem.at[0], recv_sem=recv_sem.at[n],
                 device_id={"mp": to * PLANE + rank}, device_id_type=MESH,
             ).start()
         pltpu.make_async_copy(middle.at[:, plane], dst.at[plane], recv_sem.at[n]).start()
@@ -182,7 +183,7 @@
             to = (plane + d) % PLANES
             pltpu.make_async_remote_copy(
                 src_ref=src.at[to], dst_ref=middle.at[plane],
-                send_sem=send_sem.at[n], recv_sem=recv_sem.at[n],
+                send_sem=send_sem.at[0], recv_sem=recv_sem.at[n],
                 device_id={"mp": to * PLANE + rank}, device_id_type=MESH,
             ).start()
         pltpu.make_async_copy(src.at[plane], middle.at[plane], recv_sem.at[n]).start()
@@ -192,7 +193,7 @@
             to = (rank + d) % PLANE
             pltpu.make_async_remote_copy(
                 src_ref=middle.at[:, to], dst_ref=dst.at[:, rank],
-                send_sem=send_sem.at[n], recv_sem=recv_sem.at[n],
+                send_sem=send_sem.at[0], recv_sem=recv_sem.at[n],
                 device_id={"mp": plane * PLANE + to}, device_id_type=MESH,
             ).start()
             return carry
@@ -203,7 +204,7 @@
     def to_near(src, dst, slots, n):
         for slot, offset in slots:
             pltpu.make_async_remote_copy(
-                src_ref=src, dst_ref=dst.at[slot], send_sem=send_sem.at[n],
+                src_ref=src, dst_ref=dst.at[slot], send_sem=send_sem.at[0],
                 recv_sem=recv_sem.at[n],
                 device_id={"mp": (q - offset + MP) % MP}, device_id_type=MESH,
             ).start()
@@ -212,7 +213,7 @@
         pltpu.make_async_copy(ref, ref, recv_sem.at[n]).wait()
 
     def sent(ref, n):
-        pltpu.make_async_copy(ref, ref, send_sem.at[n]).wait()
+        pltpu.make_async_copy(ref, ref, send_sem.at[0]).wait()
 
     to_plane(a1_send, a1_mid, 0)
     line_first(f_send, f_mid, 1)
@@ -271,7 +272,7 @@
             to = (e + d) % ENS
             pltpu.make_async_remote_copy(
                 src_ref=src.at[to], dst_ref=dst.at[slot],
-                send_sem=send_sem.at[n], recv_sem=recv_sem.at[n],
+                send_sem=send_sem.at[0], recv_sem=recv_sem.at[n],
                 device_id={"ens": to}, device_id_type=MESH,
             ).start()
 
@@ -323,9 +324,9 @@
     inc_v[:, 128:256] = total[8:16]
     inc_far_s[0] = inc_v[4:6, :]
     inc_far_s[1] = inc_v[0:2, :]
-    to_near(inc_v, halo_recv, ((0, -1), (1, 1)), 5)
     to_near(inc_far_s.at[0], halo_far, ((0, -2),), 14)
     to_near(inc_far_s.at[1], halo_far, ((1, 2),), 14)
+    to_near(inc_v, halo_recv, ((0, -1), (1, 1)), 5)
     arrived(rs2_recv, 12)
     total = part2_s[e].astype(F32)
     for d in range(ENS - 1):
@@ -411,7 +412,7 @@
     for d in LEVEL_ORDER:
         pltpu.make_async_remote_copy(
             src_ref=ag_send, dst_ref=ag_recv.at[e],
-            send_sem=send_sem.at[7], recv_sem=recv_sem.at[7],
+            send_sem=send_sem.at[0], recv_sem=recv_sem.at[7],
             device_id={"ens": (e + d) % ENS}, device_id_type=MESH,
         ).start()
     pltpu.make_async_copy(ag_send, ag_recv.at[e], recv_sem.at[7]).start()
@@ -574,8 +575,8 @@
         pltpu.VMEM((2, 8, WIDE), BF16),
         pltpu.VMEM((TROWS, WIDE), F32),
         pltpu.VMEM((5, TROWS, WIDE), F32),
-        pltpu.SemaphoreType.DMA((8,)),
-        pltpu.SemaphoreType.DMA((15,)),
+        pltpu.SemaphoreType.DMA((4,)),
+        pltpu.SemaphoreType.DMA((1,)),
         pltpu.SemaphoreType.DMA((15,)),
     ]
     gradient, departures = pl.pallas_call(

time: 45.5 us -> 45.2 us (level)
  no operation moved by 1% of the time
where the time goes in v6:
time: 45.2 us; the launch traced here: 45.1 us
  Pallas kernels  44.4 us (98%)
  between operations  0.64 us (1%)
    pallas_call x1, Pallas kernels, shards(): pl.pallas_call(body, out_shape=outs, in_specs=[anywhere] * len(operands),...  43.8 us

profile of v6, /device:TPU:56, one launch (start us, length us, event | category | flops | bytes accessed | tf_op | source)
XLA Modules:
  0.0 45.1 jit_solution(11528492004423522944)
XLA Ops:
  0.6 43.8 %assimilate.1 = (f32[96,192]{1,0:T(8,128)S(1)}, f32[16,128]{1,0:T(8,128)S(1)}) custom-call(bf16[64,288]{1,0:T(8,128)(2,1)} %bitcast.15, bf16[96,192]{1,0:T(8,128)(2,1)} %bitcast.16, s32[1,192]{1,0:T(1,128)} %bitcast.19, bf16[64,288]{1,0:T(8,128)(2,1)} %bitcast.17, bf16[64,288]{1,0:T(8,128)(2,1)} %bitcast.18, s32[4,4,128]{2,1,0:T(4,128)} %lon_hbm.1, ...), custom_call_target="tpu_custom_call" | custom-call | tf_op jit(solution)/shard_map/assimilate/pallas_call | solution.py:582
  44.4 0.7 %move_out.1 = (f32[96,192]{1,0:T(8,128)}, f32[16,128]{1,0:T(8,128)}) custom-call(f32[96,192]{1,0:T(8,128)S(1)} %get-tuple-element.6.grad_v, f32[16,128]{1,0:T(8,128)S(1)} %get-tuple-element.7.dep_v), custom_call_target="tpu_custom_call" | custom-call | tf_op jit(solution)/shard_map/move_out/pallas_call | solution.py:593
